TPU v7x, 32 devices: a whole 2x2x4 slice. The times are simulated.
32 devices in a mesh: grp: 2 (over y), gx: 4 (over z), gy: 2 (over x), gz: 2 (over core).
Axes of the slice: x: 2, y: 2, z: 4, core: 2. Of those that a mesh axis runs over, the one named last changes fastest.
Arguments:
- alignment_token_ids: int32 [128, 128], P(('grp', 'gx'), ('gy', 'gz')), parts along dimension 0, may hold values from 0 to 22
- homolog_profile: bfloat16 [128, 128, 256], P(('grp', 'gx'), ('gy', 'gz')), parts along dimension 0, may hold values from -6 to 6
- alignment_mask: int32 [128, 128], P(('grp', 'gx'), ('gy', 'gz')), parts along dimension 0, may hold values 0 or 1
- pair_features: bfloat16 [256, 128, 128], P(('grp', 'gy', 'gz'), 'gx'), parts along dimension 0, may hold values from -4 to 6
- symbol_lookup_weights: bfloat16 [23, 256], replicated, may hold values from -6 to 6
- asking_weights: bfloat16 [256, 256], replicated, may hold values from -0.375 to 0.375
- lookup_weights: bfloat16 [256, 256], replicated, may hold values from -0.375 to 0.375
- content_weights: bfloat16 [256, 256], replicated, may hold values from -0.375 to 0.375
- sigmoid_switch_weights: bfloat16 [256, 256], replicated, may hold values from -0.375 to 0.375
- resulting_weights: bfloat16 [256, 256], replicated, may hold values from -0.75 to 0.75
- pair_bias_matrix: float32 [128, 8], replicated, may hold values from -0.9 to 48
- first_factor_weights: bfloat16 [256, 32], replicated, may hold values from -0.375 to 0.375
- second_factor_weights: bfloat16 [256, 32], replicated, may hold values from -0.375 to 0.375
- outer_mixing_weight: bfloat16 [1024, 128], replicated, may hold values from -1 to 1
- widening_weight: bfloat16 [128, 512], replicated, may hold values from -0.5 to 0.5
- narrowing_weight: bfloat16 [512, 128], replicated, may hold values from -0.375 to 0.375
Outputs:
- profile_refreshed: bfloat16 [128, 128, 256], P(('grp', 'gx'), ('gy', 'gz')), parts along dimension 0
- pair_output: bfloat16 [256, 128, 128], P(('grp', 'gy', 'gz'), 'gx'), parts along dimension 0
There are 2 independent parts, one for each index of `grp`. A program takes and returns all parts, laid end to end along the dimension named above; an argument that names none is the same for every part. Nothing has to cross between parts.
All inputs are finite; a program needn't handle non-finite values. No bound on the sum of `alignment_mask` on one device may be relied on, other than what follows from the above.
Results may differ from a plain program's by a relative error of at most 0.013.
Values may be sent and summed in bfloat16 or wider, within the bound.
No kernel may reach another device: no remote copies, remote signals or barrier semaphores. Data moves between devices by JAX's collectives and lax.ppermute only.
A program may use at most 64 MiB of HBM per device.

v0:
```python
import functools
import math

import jax
import jax.numpy as jnp
from jax import lax
from jax.experimental import pallas as pl
from jax.experimental.pallas import tpu as pltpu
from jax.sharding import PartitionSpec as P


LANES = 128
UNROLL = 4
F32 = jnp.float32
BF16 = jnp.bfloat16


def iota(shape, dim):
    return lax.broadcasted_iota(jnp.int32, shape, dim)


def standardize(values):
    average = jnp.mean(values, axis=-1, keepdims=True)
    centred = values - average
    return centred * lax.rsqrt(jnp.mean(centred * centred, axis=-1, keepdims=True) + 1e-05)


def dot(left, right, contract=(1, 0), precision=None):
    return lax.dot_general(
        left,
        right,
        (((contract[0],), (contract[1],)), ((), ())),
        preferred_element_type=F32,
        precision=precision,
    )


def tiling_matrix(rows, columns):
    return (iota((rows, columns), 1) % rows == iota((rows, columns), 0)).astype(BF16)


def call(body, outs, scratch=(), flops=0, data=0, far=0):
    near = pl.BlockSpec(memory_space=pltpu.VMEM)
    held = sum(
        math.prod(ref.shape) * jnp.dtype(ref.dtype).itemsize
        for ref in scratch
        if hasattr(ref, "shape") and ref.memory_space == pltpu.VMEM
    )

    def run(*operands):
        operands = [
            pltpu.with_memory_space_constraint(x, pltpu.HBM) if n < far else x
            for n, x in enumerate(operands)
        ]
        return pl.pallas_call(
            body,
            out_shape=outs,
            in_specs=[pl.BlockSpec(memory_space=pltpu.HBM)] * far + [near] * (len(operands) - far),
            out_specs=jax.tree.map(lambda _: near, outs),
            scratch_shapes=scratch,
            cost_estimate=pl.CostEstimate(flops=flops, bytes_accessed=data, transcendentals=0),
            compiler_params=pltpu.CompilerParams(vmem_limit_bytes=held * 5 // 4 + (4 << 20)),
        )(*operands)

    return run


def fetch(sources, targets, sems):
    copies = [
        pltpu.make_async_copy(source, target, sems.at[n])
        for n, (source, target) in enumerate(zip(sources, targets))
    ]
    for copy in copies:
        copy.start()
    return copies


def embed_kernel(
    ids_far,
    mask_far,
    profile_far,
    table_far,
    pair_far,
    msg_ref,
    arriving_ref,
    mask_ref,
    pair_ref,
    ids_ref,
    profile_ref,
    table_ref,
    padded,
    sems,
):
    copies = fetch(
        (ids_far, table_far, mask_far, profile_far, pair_far),
        (ids_ref, table_ref, mask_ref, profile_ref, pair_ref),
        sems,
    )
    sequences, residues, features = profile_ref.shape
    kinds = table_ref.shape[0]
    for copy in copies[:3]:
        copy.wait()
    padded[...] = jnp.zeros_like(padded)
    padded[0:kinds, :] = table_ref[...]
    columns = ids_ref[...].astype(F32).T
    labels = iota((residues, padded.shape[0]), 1).astype(F32)
    rows = sequences * residues
    mask = mask_ref[...].astype(F32).astype(BF16)
    msg_ref[rows:, :] = dot(mask, tiling_matrix(residues, features)).astype(BF16)
    table = padded[...]
    copies[3].wait()
    step = 4
    for start in range(0, sequences, step):
        hot = [
            (columns[:, s : s + 1] == labels).astype(F32).astype(BF16)
            for s in range(start, start + step)
        ]
        where = slice(start * residues, (start + step) * residues)
        profile = profile_ref[start : start + step].reshape(step * residues, features)
        arriving = profile.astype(F32) + dot(jnp.concatenate(hot, axis=0), table)
        arriving_ref[where, :] = arriving
        msg_ref[where, :] = standardize(arriving).astype(BF16)
    copies[4].wait()


def prepare_kernel(weights, *refs):
    far, pair_ref, refs = refs[:weights], refs[weights], refs[weights + 1 :]
    near, (out_ref, matrix_ref, sems) = refs[: weights - 1], refs[weights - 1 :]
    copies = fetch(far[-1:] + far[:-1], (matrix_ref,) + near, sems)
    rows, columns, width = pair_ref.shape
    copies[0].wait()
    matrix = matrix_ref[...]
    step = LANES // columns
    for start in range(0, rows, step):
        part = pair_ref[start : start + step].reshape(step * columns, width).astype(F32)
        out_ref[:, start * columns : (start + step) * columns] = dot(
            matrix, standardize(part), (1, 1), lax.Precision.HIGHEST
        )
    for copy in copies[1:]:
        copy.wait()


def block_kernel(mix_ref, block_ref, wide):
    width = other = math.isqrt(mix_ref.shape[0])
    pair_width = mix_ref.shape[1]
    fit = LANES // width
    wide[...] = mix_ref[...].astype(F32)
    blank = jnp.zeros((width, pair_width), BF16)
    for d in range(other):
        piece = wide[pl.ds(d, width, stride=other), :].astype(BF16)
        for p in range(fit):
            spot = slice((d * fit + p) * width, (d * fit + p + 1) * width)
            for q in range(fit):
                block_ref[spot, q * pair_width : (q + 1) * pair_width] = (
                    piece if q == p else blank
                )


def project_kernel(position, *refs):
    blocks = len(position)
    msgs = refs[:blocks]
    wq_ref, wk_ref, wv_ref, wg_ref, q_ref, k_ref, v_ref, g_ref, pen_ref = refs[blocks:]
    sequences, residues, _ = q_ref.shape
    rows = sequences * residues
    total = pen_ref.shape[1]
    x_own, c_own = lax.axis_index("gy"), lax.axis_index("gz")
    own = msgs[0][0:rows, :]
    q_ref[...] = dot(own, wq_ref[...]).astype(BF16).reshape(q_ref.shape)
    g_ref[...] = jax.nn.sigmoid(dot(own, wg_ref[...])).reshape(g_ref.shape)
    lane_block = iota((sequences, total), 1) // residues
    present = jnp.zeros((sequences, total), F32)
    for msg, (shift_y, shift_z, size_y, size_z) in zip(msgs, position):
        block = lax.rem(x_own - shift_y + size_y, size_y) * size_z + lax.rem(
            c_own - shift_z + size_z, size_z
        )
        where = pl.ds(pl.multiple_of(block * residues, residues), residues)
        normed = msg[0:rows, :]
        k_ref[:, where, :] = dot(normed, wk_ref[...]).astype(BF16).reshape(q_ref.shape)
        v_ref[:, where, :] = dot(normed, wv_ref[...]).astype(BF16).reshape(q_ref.shape)
        tiled = msg[rows : rows + sequences, :].astype(F32)
        while tiled.shape[1] < total:
            tiled = jnp.concatenate([tiled, tiled], axis=1)
        present = jnp.where(lane_block == block, tiled[:, 0:total], present)
    pen_ref[...] = (present - 1.0) * 1000000000.0


def attend_kernel(heads, groups, *refs):
    biases, refs = refs[:groups], refs[groups:]
    attend_body(heads, biases, *refs)


def attend_body(
    heads,
    biases,
    q_ref,
    k_ref,
    v_ref,
    g_ref,
    pen_ref,
    arriving_ref,
    mask_ref,
    wr_ref,
    wf_ref,
    ws_ref,
    profile_ref,
    left_ref,
    right_ref,
    bias_ref,
    spread,
    bias,
    scored,
    weighed,
    belows,
    gated,
    leftish,
    rightish,
):
    sequences, residues, features = q_ref.shape
    total = k_ref.shape[1]
    size = features // heads
    per = LANES // size
    fit = LANES // residues
    z_own = lax.axis_index("gx")
    for other, ref in enumerate(biases):
        bias_ref[z_own ^ other] = ref[...]
    lane = iota((heads, LANES), 1) // residues
    for i in range(residues):
        tile, inner = divmod(i, fit)
        for column in range(total // LANES):
            value = None
            for slot in range(fit):
                source = bias_ref[
                    column * fit + slot, :, tile * LANES : (tile + 1) * LANES
                ]
                shift = ((slot - inner) % fit) * residues
                if shift:
                    source = pltpu.roll(source, shift, 1)
                value = source if value is None else jnp.where(lane == slot, source, value)
            spread[column, i * heads : (i + 1) * heads, :] = value
    for column in range(total // LANES):
        for h in range(heads):
            bias[
                h * residues : (h + 1) * residues, column * LANES : (column + 1) * LANES
            ] = spread[column, pl.ds(h, residues, stride=heads), :]
    scale = size ** (-0.5)
    span = per * residues
    own_lanes = iota((span, LANES), 0) // residues == iota((span, LANES), 1) // size
    small_lanes = [iota((residues, LANES), 1) // size == p for p in range(per)]
    parts = [
        (slice(part * LANES, (part + 1) * LANES), slice(part * span, (part + 1) * span))
        for part in range(heads // per)
    ]

    def score(s, carry):
        penalty = pen_ref[pl.ds(s, 1), :]
        for lanes, span_rows in parts:
            query = q_ref[s, :, lanes]
            stacked = jnp.concatenate([query] * per, axis=0)
            stacked = jnp.where(own_lanes, stacked, jnp.zeros_like(stacked))
            scores = dot(stacked, k_ref[s, :, lanes], (1, 1)) * scale
            scored[s, span_rows, :] = scores + bias[span_rows, :] + penalty
        return carry

    def weigh(s, carry):
        for lanes, span_rows in parts:
            scores = scored[s, span_rows, :]
            top = jnp.max(scores, axis=1, keepdims=True)
            weights = jnp.exp(scores - top)
            aggregate = jnp.sum(weights, axis=1, keepdims=True)
            weighed[s, span_rows, :] = weights.astype(BF16)
            below = jnp.broadcast_to(aggregate[0:residues, :], (residues, LANES))
            for p in range(1, per):
                rows = slice(p * residues, (p + 1) * residues)
                below = jnp.where(small_lanes[p], aggregate[rows, :], below)
            belows[s, :, lanes] = g_ref[s, :, lanes] / below
        return carry

    def gather(s, carry):
        for lanes, span_rows in parts:
            mixed = dot(weighed[s, span_rows, :], v_ref[s, :, lanes])
            value = mixed[0:residues, :]
            for p in range(1, per):
                rows = slice(p * residues, (p + 1) * residues)
                value = jnp.where(small_lanes[p], mixed[rows, :], value)
            gated[s, :, lanes] = (belows[s, :, lanes] * value).astype(BF16)
        return carry

    for stage in (score, weigh, gather):
        lax.fori_loop(0, sequences, stage, 0, unroll=UNROLL)

    rows = sequences * residues
    refreshed = (
        arriving_ref[...] + dot(gated[...].reshape(rows, features), wr_ref[...])
    ).astype(BF16)
    profile_ref[...] = refreshed.reshape(profile_ref.shape)
    normed = standardize(refreshed.astype(F32)).astype(BF16)
    leftish[...] = dot(normed, jnp.concatenate([wf_ref[...]] * (LANES // wf_ref.shape[0])), (1, 1))
    width = ws_ref.shape[0]
    for s in range(sequences):
        piece = normed[s * residues : (s + 1) * residues, :]
        rightish[s * width : (s + 1) * width, :] = dot(
            ws_ref[...], jnp.concatenate([piece] * fit, axis=0), (1, 1)
        )
    mask = mask_ref[...].astype(F32).astype(BF16)
    wide = residues * width
    expand = (iota((residues, wide), 1) // width == iota((residues, wide), 0)).astype(BF16)
    left_mask = dot(mask, expand)
    right_mask = dot(mask, tiling_matrix(residues, width * residues))
    for tile in range(wide // LANES):
        lanes = slice(tile * LANES, (tile + 1) * LANES)
        for source, stride, step, target, present in (
            (leftish, residues, width, left_ref, left_mask),
            (rightish, width, residues, right_ref, right_mask),
        ):
            group = iota((sequences, LANES), 1) // step
            count = LANES // step
            value = source[pl.ds(tile * count, sequences, stride=stride), :]
            for p in range(1, count):
                other = source[pl.ds(tile * count + p, sequences, stride=stride), :]
                value = jnp.where(group == p, other, value)
            target[:, lanes] = (value * present[:, lanes]).astype(BF16)
    left_ref[:, wide:] = right_mask[:, 0:LANES].astype(BF16)
    right_ref[:, wide:] = right_mask[:, 0:LANES].astype(BF16)


def pair_kernel(left_from, right_from, *refs):
    lefts = refs[: len(left_from)]
    rights = refs[len(left_from) : len(left_from) + len(right_from)]
    (pair_ref, block_ref, w1_ref, w2_ref, out_ref, left, right, stacked, middle) = refs[
        len(left_from) + len(right_from) :
    ]
    sequences = lefts[0].shape[0]
    rows, columns, pair_width = pair_ref.shape
    z_own, x_own, c_own = (lax.axis_index(n) for n in ("gx", "gy", "gz"))
    for ref, other in zip(lefts, left_from):
        start = (z_own ^ other) * sequences
        left[pl.ds(pl.multiple_of(start, sequences), sequences), :] = ref[...]
    for ref, (shift_y, shift_z, size_y, size_z) in zip(rights, right_from):
        block = lax.rem(x_own - shift_y + size_y, size_y) * size_z + lax.rem(
            c_own - shift_z + size_z, size_z
        )
        right[pl.ds(pl.multiple_of(block * sequences, sequences), sequences), :] = ref[...]
    wide = left.shape[1] - LANES
    width = wide // rows
    fit = LANES // width
    depth = wide // columns
    count = dot(right[:, wide:], left[:, wide:], (0, 0))[0:columns, :]
    share = 1.0 / (count + 1.0)
    flipped = right[:, 0:wide].T
    tiles = wide // LANES
    pack = 2 if tiles % 2 == 0 else 1
    for start in range(0, tiles, pack):
        outer = dot(flipped, left[:, start * LANES : (start + pack) * LANES]).astype(BF16)
        for q in range(pack):
            for d in range(depth):
                stacked[
                    (start + q) * columns : (start + q + 1) * columns,
                    d * LANES : (d + 1) * LANES,
                ] = outer[d * columns : (d + 1) * columns, q * LANES : (q + 1) * LANES]
    mixed = dot(stacked[...], block_ref[...])
    for i in range(rows):
        tile, inner = divmod(i, fit)
        part = mixed[
            tile * columns : (tile + 1) * columns,
            inner * pair_width : (inner + 1) * pair_width,
        ]
        middle[i] = pair_ref[i].astype(F32) + part * share[:, i : i + 1]
    flat = middle[...].reshape(rows * columns, pair_width)
    normed = standardize(flat).astype(BF16)
    hidden = jnp.maximum(dot(normed, w1_ref[...]), 0.0).astype(BF16)
    out_ref[...] = (flat + dot(hidden, w2_ref[...])).astype(BF16).reshape(out_ref.shape)


def local(
    sizes,
    alignment_token_ids,
    homolog_profile,
    alignment_mask,
    pair_features,
    symbol_lookup_weights,
    asking_weights,
    lookup_weights,
    content_weights,
    sigmoid_switch_weights,
    resulting_weights,
    pair_bias_matrix,
    first_factor_weights,
    second_factor_weights,
    outer_mixing_weight,
    widening_weight,
    narrowing_weight,
):
    size_x, size_y, size_z = sizes
    sequences, residues, features = homolog_profile.shape
    heads = pair_bias_matrix.shape[1]
    width = first_factor_weights.shape[1]
    pair_rows, pair_columns, pair_width = pair_features.shape
    total = residues * size_y * size_z
    rows = sequences * residues
    shape = jax.ShapeDtypeStruct

    local_pair = shape(pair_features.shape, BF16)
    local_mask = shape(alignment_mask.shape, jnp.int32)
    msg, arriving, mask, pair = call(
        embed_kernel,
        (
            shape((rows + sequences, features), BF16),
            shape((rows, features), F32),
            local_mask,
            local_pair,
        ),
        [
            pltpu.VMEM(alignment_token_ids.shape, jnp.int32),
            pltpu.VMEM(homolog_profile.shape, BF16),
            pltpu.VMEM(symbol_lookup_weights.shape, BF16),
            pltpu.VMEM((LANES, features), BF16),
            pltpu.SemaphoreType.DMA((5,)),
        ],
        flops=2 * rows * LANES * features,
        data=rows * features * 8,
        far=5,
    )(
        alignment_token_ids,
        alignment_mask,
        homolog_profile,
        symbol_lookup_weights,
        pair_features,
    )

    def shift(value, axis, count, step):
        return lax.ppermute(value, axis, [(n, (n + step) % count) for n in range(count)])

    far = [msg] + [shift(msg, "gy", size_y, r) for r in range(1, size_y)]
    position, msgs = [], []
    for r in range(size_y):
        for t in range(size_z):
            position.append((r, t, size_y, size_z))
            msgs.append(far[r] if t == 0 else shift(far[r], "gz", size_z, t))

    fit = LANES // width
    weights = (
        asking_weights,
        lookup_weights,
        content_weights,
        sigmoid_switch_weights,
        resulting_weights,
        first_factor_weights.T,
        second_factor_weights.T,
        widening_weight,
        narrowing_weight,
        outer_mixing_weight,
    )
    wq, wk, wv, wg, wr, wf, ws, w1, w2, mix, bias_local = call(
        functools.partial(prepare_kernel, len(weights) + 1),
        tuple(shape(w.shape, w.dtype) for w in weights)
        + (shape((heads, pair_rows * pair_columns), F32),),
        [
            pltpu.VMEM(pair_bias_matrix.T.shape, F32),
            pltpu.SemaphoreType.DMA((len(weights) + 1,)),
        ],
        flops=2 * 6 * pair_rows * pair_columns * pair_width * LANES,
        data=pair_rows * pair_columns * pair_width * 2,
        far=len(weights) + 1,
    )(*weights, pair_bias_matrix.T, pair)
    biases = [bias_local] + [
        lax.ppermute(bias_local, "gx", [(n, n ^ m) for n in range(size_x)])
        for m in range(1, size_x)
    ]

    three = (sequences, residues, features)
    keys = (sequences, total, features)
    queries, keys, values, gates, penalty = call(
        functools.partial(project_kernel, tuple(position)),
        (
            shape(three, BF16),
            shape(keys, BF16),
            shape(keys, BF16),
            shape(three, F32),
            shape((sequences, total), F32),
        ),
        flops=2 * sequences * (total + residues) * features * features * 2,
        data=sequences * total * features * 6,
    )(*msgs, wq, wk, wv, wg)

    wide = residues * width
    message = shape((sequences, wide + LANES), BF16)
    refreshed, left_own, right_own = call(
        functools.partial(attend_kernel, heads, size_x),
        (shape(three, BF16), message, message),
        [
            pltpu.VMEM((size_x, heads, pair_rows * pair_columns), F32),
            pltpu.VMEM((total // LANES, residues * heads, LANES), F32),
            pltpu.VMEM((heads * residues, total), F32),
            pltpu.VMEM((sequences, heads * residues, total), F32),
            pltpu.VMEM((sequences, heads * residues, total), BF16),
            pltpu.VMEM(three, F32),
            pltpu.VMEM(three, BF16),
            pltpu.VMEM((rows, LANES), F32),
            pltpu.VMEM((sequences * width, LANES), F32),
        ],
        flops=4 * sequences * heads * residues * total * LANES,
        data=sequences * total * features * 4,
    )(*biases, queries, keys, values, gates, penalty, arriving, mask, wr, wf, ws)

    lefts = [left_own] + [
        lax.ppermute(left_own, "gx", [(n, n ^ m) for n in range(size_x)])
        for m in range(1, size_x)
    ]
    right_from, rights = [], []
    blocks = size_y * size_z
    for r in range(size_y):
        pairs = []
        for a in range(size_x):
            for b in range(blocks):
                to = ((a // size_z + r) % size_y) * size_z + a % size_z
                pairs.append((a * blocks + b, b * blocks + to))
        got = lax.ppermute(right_own, ("gx", "gy", "gz"), pairs)
        for t in range(size_z):
            right_from.append((r, t, size_y, size_z))
            rights.append(got if t == 0 else shift(got, "gz", size_z, t))

    block = call(
        block_kernel,
        shape((width * width * fit, pair_width * fit), BF16),
        [pltpu.VMEM(outer_mixing_weight.shape, F32)],
        data=width * width * fit * pair_width * fit * 2,
    )(mix)

    depth = sequences * size_x
    pair_output = call(
        functools.partial(pair_kernel, tuple(range(size_x)), tuple(right_from)),
        shape(pair_features.shape, BF16),
        [
            pltpu.VMEM((depth, wide + LANES), BF16),
            pltpu.VMEM((depth, wide + LANES), BF16),
            pltpu.VMEM((pair_rows // fit * pair_columns, width * LANES), BF16),
            pltpu.VMEM(pair_features.shape, F32),
        ],
        flops=2 * pair_rows * pair_columns * width * width * pair_width * fit,
        data=width * width * fit * pair_width * fit * 2,
    )(*lefts, *rights, pair, block, w1, w2)
    return refreshed, pair_output


def solution(mesh):
    sizes = tuple(mesh.shape[name] for name in ("gx", "gy", "gz"))
    assert sizes[0] == sizes[1] * sizes[2] and sizes[0] & (sizes[0] - 1) == 0
    in_specs = (
        P(("grp", "gx"), ("gy", "gz")),
        P(("grp", "gx"), ("gy", "gz"), None),
        P(("grp", "gx"), ("gy", "gz")),
        P(("grp", "gy", "gz"), "gx", None),
    ) + (P(),) * 12
    out_specs = (P(("grp", "gx"), ("gy", "gz"), None), P(("grp", "gy", "gz"), "gx", None))

    def body(*args):
        return local(sizes, *args)

    return jax.shard_map(
        body, mesh=mesh, in_specs=in_specs, out_specs=out_specs, check_vma=False
    )
```

profile of v0, /device:TPU:0, one launch (start us, length us, event | category | flops | bytes accessed | tf_op | source)
XLA Modules:
  0.0 44.9 jit_solution(9271796812982948681)
XLA Ops:
  0.6 1.5 %shard_map.167 = (bf16[528,256]{1,0:T(8,128)(2,1)S(1)}, f32[512,256]{1,0:T(8,128)S(1)}, s32[16,32]{1,0:T(8,128)S(1)}, bf16[32,32,128]{2,1,0:T(8,128)(2,1)S(1)}) custom-call(s32[16,32]{1,0:T(8,128)} %ids_far.1, s32[16,32]{1,0:T(8,128)} %mask_far.1, bf16[16,32,256]{2,1,0:T(8,128)(2,1)} %profile_far.1, bf16[23,256]{1,0:T(8,128)(2,1)} %table_far.1, ...), custom_call_target="tpu_custom_call" | custom-call | flops 33554432 | bytes 1048576 | tf_op jit(solution)/shard_map/pallas_call | solution.py:55
  2.1 3.0 %collective-permute-start.4 = (bf16[528,256]{1,0:T(8,128)(2,1)S(1)}, bf16[528,256]{1,0:T(8,128)(2,1)S(1)}, u32[]{:S(2)}, u32[]{:S(2)}) collective-permute-start(bf16[528,256]{1,0:T(8,128)(2,1)S(1)} %get-tuple-element.27.refs_0_), channel_id=1, source_target_pairs={{0,2},{2,0},{1,3},{3,1},{4,6},{6,4},{5,7},{7,5},{8,10},{10,8},{9,1... | collective-permute-start | bytes 811016 | tf_op jit(solution)/shard_map/ppermute | solution.py:431
  5.2 0.0 collective-permute-start.3
  5.2 6.5 %collective-permute-done.4.refs_2_ = bf16[528,256]{1,0:T(8,128)(2,1)S(1)} collective-permute-done((bf16[528,256]{1,0:T(8,128)(2,1)S(1)}, bf16[528,256]{1,0:T(8,128)(2,1)S(1)}, u32[]{:S(2)}, u32[]{:S(2)}) %collective-permute-start.4) | collective-permute-done | bytes 270368 | tf_op jit(solution)/shard_map/ppermute | solution.py:431
  11.7 0.0 collective-permute-start.5
  11.7 1.9 %shard_map.168 = (bf16[256,256]{1,0:T(8,128)(2,1)S(1)}, bf16[256,256]{1,0:T(8,128)(2,1)S(1)}, bf16[256,256]{1,0:T(8,128)(2,1)S(1)}, bf16[256,256]{1,0:T(8,128)(2...) custom-call(bf16[256,256]{1,0:T(8,128)(2,1)} %refs_0_.1, ...), custom_call_target="tpu_custom_call" | custom-call | flops 201326592 | bytes 262144 | tf_op jit(solution)/shard_map/pallas_call | solution.py:55
  13.6 1.9 %collective-permute-start = (f32[8,1024]{1,0:T(8,128)S(1)}, f32[8,1024]{1,0:T(8,128)S(1)}, u32[]{:S(2)}, u32[]{:S(2)}) collective-permute-start(f32[8,1024]{1,0:T(8,128)S(1)} %get-tuple-element.26.refs_0_), channel_id=1, source_target_pairs={{0,4},{4,0},{8,12},{12,8},{1,5},{5,1},{9,13},{13,9},{2,6},{6,2},{1... | collective-permute-start | bytes 98312 | tf_op jit(solution)/shard_map/ppermute | solution.py:466
  15.5 2.6 %collective-permute-start.1 = (f32[8,1024]{1,0:T(8,128)S(1)}, f32[8,1024]{1,0:T(8,128)S(1)}, u32[]{:S(2)}, u32[]{:S(2)}) collective-permute-start(f32[8,1024]{1,0:T(8,128)S(1)} %get-tuple-element.26.refs_0_), channel_id=1, source_target_pairs={{0,8},{4,12},{8,0},{12,4},{1,9},{5,13},{9,1},{13,5},{2,10},{6,14},... | collective-permute-start | bytes 98312 | tf_op jit(solution)/shard_map/ppermute | solution.py:466
  18.1 0.0 collective-permute-start.2
  18.1 0.0 collective-permute-done.3.refs_1_
  18.1 0.0 collective-permute-done.5.refs_3_
  18.1 0.9 %shard_map.169 = (bf16[16,32,256]{2,1,0:T(8,128)(2,1)S(1)}, bf16[16,128,256]{2,1,0:T(8,128)(2,1)S(1)}, bf16[16,128,256]{2,1,0:T(8,128)(2,1)S(1)}, f32[16,32,256]{2,1,0:T(8,128)S(1)}, f32[16,128]{1,0:T(8,128)S(1)}) custom-call(bf16[528,256]{1,0:T(8,128)(2,1)S(1)} %get-tuple-element.27.refs_0_, bf16[528,256]{1,0:T(8,128)(2,1)S(1)} %collective-permute-done.3.refs_1_, ...), custom_call_target="tpu_custom_call" | custom-call | flops 671088640 | bytes 3145728 | tf_op jit(solution)/shard_map/pallas_call | solution.py:55
  18.9 0.0 collective-permute-done.refs_1_
  18.9 1.9 %collective-permute-done.1.refs_2_ = f32[8,1024]{1,0:T(8,128)S(1)} collective-permute-done((f32[8,1024]{1,0:T(8,128)S(1)}, f32[8,1024]{1,0:T(8,128)S(1)}, u32[]{:S(2)}, u32[]{:S(2)}) %collective-permute-start.1) | collective-permute-done | bytes 32800 | tf_op jit(solution)/shard_map/ppermute | solution.py:466
  20.8 3.0 %collective-permute-done.2.refs_3_ = f32[8,1024]{1,0:T(8,128)S(1)} collective-permute-done((f32[8,1024]{1,0:T(8,128)S(1)}, f32[8,1024]{1,0:T(8,128)S(1)}, u32[]{:S(2)}, u32[]{:S(2)}) %collective-permute-start.2) | collective-permute-done | bytes 32800 | tf_op jit(solution)/shard_map/ppermute | solution.py:466
  23.8 5.8 %shard_map.170 = (bf16[16,32,256]{2,1,0:T(8,128)(2,1)}, bf16[16,1152]{1,0:T(8,128)(2,1)S(1)}, bf16[16,1152]{1,0:T(8,128)(2,1)S(1)}) custom-call(f32[8,1024]{1,0:T(8,128)S(1)} %get-tuple-element.26.refs_0_, f32[8,1024]{1,0:T(8,128)S(1)} %collective-permute-done.refs_1_, f32[8,1024]{1,0:T(8,128)S(1)} %collective-permute-done.1.refs_2_, ...), custom_call_target="tpu_custom_call" | custom-call | flops 268435456 | bytes 2097152 | tf_op jit(solution)/shard_map/pallas_call | solution.py:55
  29.6 0.7 %collective-permute-start.9 = (bf16[16,1152]{1,0:T(8,128)(2,1)S(1)}, bf16[16,1152]{1,0:T(8,128)(2,1)S(1)}, u32[]{:S(2)}, u32[]{:S(2)}) collective-permute-start(bf16[16,1152]{1,0:T(8,128)(2,1)S(1)} %get-tuple-element.44), channel_id=1, source_target_pairs={{0,0},{1,4},{2,8},{3,12},{4,1},{5,5},{6,9},{7,13},{8,2},{9,6},{10,... | collective-permute-start | bytes 110600 | tf_op jit(solution)/shard_map/ppermute | solution.py:517
  30.2 2.8 %collective-permute-start.11 = (bf16[16,1152]{1,0:T(8,128)(2,1)S(1)}, bf16[16,1152]{1,0:T(8,128)(2,1)S(1)}, u32[]{:S(2)}, u32[]{:S(2)}) collective-permute-start(bf16[16,1152]{1,0:T(8,128)(2,1)S(1)} %get-tuple-element.44), channel_id=1, source_target_pairs={{0,2},{1,6},{2,10},{3,14},{4,3},{5,7},{6,11},{7,15},{8,0},{9,4},{1... | collective-permute-start | bytes 110600 | tf_op jit(solution)/shard_map/ppermute | solution.py:517
  33.0 1.5 %collective-permute-start.6 = (bf16[16,1152]{1,0:T(8,128)(2,1)S(1)}, bf16[16,1152]{1,0:T(8,128)(2,1)S(1)}, u32[]{:S(2)}, u32[]{:S(2)}) collective-permute-start(bf16[16,1152]{1,0:T(8,128)(2,1)S(1)} %get-tuple-element.43.refs_0_), channel_id=1, source_target_pairs={{0,4},{4,0},{8,12},{12,8},{1,5},{5,1},{9,13},{13,9},{2,6},{6,2},{1... | collective-permute-start | bytes 110600 | tf_op jit(solution)/shard_map/ppermute | solution.py:506
  34.6 1.0 %collective-permute-start.7 = (bf16[16,1152]{1,0:T(8,128)(2,1)S(1)}, bf16[16,1152]{1,0:T(8,128)(2,1)S(1)}, u32[]{:S(2)}, u32[]{:S(2)}) collective-permute-start(bf16[16,1152]{1,0:T(8,128)(2,1)S(1)} %get-tuple-element.43.refs_0_), channel_id=1, source_target_pairs={{0,8},{4,12},{8,0},{12,4},{1,9},{5,13},{9,1},{13,5},{2,10},{6,14},... | collective-permute-start | bytes 110600 | tf_op jit(solution)/shard_map/ppermute | solution.py:506
  35.5 1.9 %collective-permute-start.8 = (bf16[16,1152]{1,0:T(8,128)(2,1)S(1)}, bf16[16,1152]{1,0:T(8,128)(2,1)S(1)}, u32[]{:S(2)}, u32[]{:S(2)}) collective-permute-start(bf16[16,1152]{1,0:T(8,128)(2,1)S(1)} %get-tuple-element.43.refs_0_), channel_id=1, source_target_pairs={{0,12},{4,8},{8,4},{12,0},{1,13},{5,9},{9,5},{13,1},{2,14},{6,10},... | collective-permute-start | bytes 110600 | tf_op jit(solution)/shard_map/ppermute | solution.py:506
  37.4 0.0 collective-permute-done.9.refs_4_
  37.4 0.0 collective-permute-start.10
  37.4 1.5 %collective-permute-done.11.refs_6_ = bf16[16,1152]{1,0:T(8,128)(2,1)S(1)} collective-permute-done((bf16[16,1152]{1,0:T(8,128)(2,1)S(1)}, bf16[16,1152]{1,0:T(8,128)(2,1)S(1)}, u32[]{:S(2)}, u32[]{:S(2)}) %collective-permute-start.11) | collective-permute-done | bytes 36896 | tf_op jit(solution)/shard_map/ppermute | solution.py:517
  38.9 0.0 collective-permute-start.12
  38.9 0.8 %shard_map.171.refs_9_ = bf16[4096,512]{1,0:T(8,128)(2,1)S(1)} custom-call(bf16[1024,128]{1,0:T(8,128)(2,1)S(1)} %get-tuple-element.45.mix_ref), custom_call_target="tpu_custom_call" | custom-call | bytes 4194304 | tf_op jit(solution)/shard_map/pallas_call | solution.py:55
  39.8 0.0 collective-permute-done.6.refs_1_
  39.8 0.0 collective-permute-done.7.refs_2_
  39.8 1.5 %collective-permute-done.8.refs_3_ = bf16[16,1152]{1,0:T(8,128)(2,1)S(1)} collective-permute-done((bf16[16,1152]{1,0:T(8,128)(2,1)S(1)}, bf16[16,1152]{1,0:T(8,128)(2,1)S(1)}, u32[]{:S(2)}, u32[]{:S(2)}) %collective-permute-start.8) | collective-permute-done | bytes 36896 | tf_op jit(solution)/shard_map/ppermute | solution.py:506
  41.3 0.0 collective-permute-done.10.refs_5_
  41.3 0.0 collective-permute-done.12.refs_7_
  41.3 3.6 %shard_map.172 = bf16[32,32,128]{2,1,0:T(8,128)(2,1)} custom-call(bf16[16,1152]{1,0:T(8,128)(2,1)S(1)} %get-tuple-element.43.refs_0_, bf16[16,1152]{1,0:T(8,128)(2,1)S(1)} %collective-permute-done.6.refs_1_, bf16[16,1152]{1,0:T(8,128)(2,1)S(1)} %collective-permute-done.7.refs_2_, bf16[16,1152]{1,0:T(8,128)(2,1)S(1)} %collective-permute-done.8.refs_3_, ...), custom_call_target="tpu_custom_call" | custom-call | flops 1073741824 | bytes 4194304 | tf_op jit(solution)/shard_map/pallas_call | solution.py:55
Async XLA Ops:
  2.1 9.5 %collective-permute-start.4 = (bf16[528,256]{1,0:T(8,128)(2,1)S(1)}, bf16[528,256]{1,0:T(8,128)(2,1)S(1)}, u32[]{:S(2)}, u32[]{:S(2)}) collective-permute-start(bf16[528,256]{1,0:T(8,128)(2,1)S(1)} %get-tuple-element.27.refs_0_), channel_id=1, source_target_pairs={{0,2},{2,0},{1,3},{3,1},{4,6},{6,4},{5,7},{7,5},{8,10},{10,8},{9,1... | collective-permute-start | bytes 811016 | tf_op jit(solution)/shard_map/ppermute | solution.py:431
  5.2 12.9 %collective-permute-start.3 = (bf16[528,256]{1,0:T(8,128)(2,1)S(1)}, bf16[528,256]{1,0:T(8,128)(2,1)S(1)}, u32[]{:S(2)}, u32[]{:S(2)}) collective-permute-start(bf16[528,256]{1,0:T(8,128)(2,1)S(1)} %get-tuple-element.27.refs_0_), channel_id=1, source_target_pairs={{0,1},{1,0},{2,3},{3,2},{4,5},{5,4},{6,7},{7,6},{8,9},{9,8},{10,11... | collective-permute-start | bytes 811016 | tf_op jit(solution)/shard_map/ppermute | solution.py:431
  11.7 6.4 %collective-permute-start.5 = (bf16[528,256]{1,0:T(8,128)(2,1)S(1)}, bf16[528,256]{1,0:T(8,128)(2,1)S(1)}, u32[]{:S(2)}, u32[]{:S(2)}) collective-permute-start(bf16[528,256]{1,0:T(8,128)(2,1)S(1)} %collective-permute-done.4.refs_2_), channel_id=1, source_target_pairs={{0,1},{1,0},{2,3},{3,2},{4,5},{5,4},{6,7},{7,6},{8,9},{9,8},{10,11... | collective-permute-start | bytes 811016 | tf_op jit(solution)/shard_map/ppermute | solution.py:431
  13.6 5.4 %collective-permute-start = (f32[8,1024]{1,0:T(8,128)S(1)}, f32[8,1024]{1,0:T(8,128)S(1)}, u32[]{:S(2)}, u32[]{:S(2)}) collective-permute-start(f32[8,1024]{1,0:T(8,128)S(1)} %get-tuple-element.26.refs_0_), channel_id=1, source_target_pairs={{0,4},{4,0},{8,12},{12,8},{1,5},{5,1},{9,13},{13,9},{2,6},{6,2},{1... | collective-permute-start | bytes 98312 | tf_op jit(solution)/shard_map/ppermute | solution.py:466
  15.5 5.3 %collective-permute-start.1 = (f32[8,1024]{1,0:T(8,128)S(1)}, f32[8,1024]{1,0:T(8,128)S(1)}, u32[]{:S(2)}, u32[]{:S(2)}) collective-permute-start(f32[8,1024]{1,0:T(8,128)S(1)} %get-tuple-element.26.refs_0_), channel_id=1, source_target_pairs={{0,8},{4,12},{8,0},{12,4},{1,9},{5,13},{9,1},{13,5},{2,10},{6,14},... | collective-permute-start | bytes 98312 | tf_op jit(solution)/shard_map/ppermute | solution.py:466
  18.1 5.7 %collective-permute-start.2 = (f32[8,1024]{1,0:T(8,128)S(1)}, f32[8,1024]{1,0:T(8,128)S(1)}, u32[]{:S(2)}, u32[]{:S(2)}) collective-permute-start(f32[8,1024]{1,0:T(8,128)S(1)} %get-tuple-element.26.refs_0_), channel_id=1, source_target_pairs={{0,12},{4,8},{8,4},{12,0},{1,13},{5,9},{9,5},{13,1},{2,14},{6,10},... | collective-permute-start | bytes 98312 | tf_op jit(solution)/shard_map/ppermute | solution.py:466
  29.6 7.9 %collective-permute-start.9 = (bf16[16,1152]{1,0:T(8,128)(2,1)S(1)}, bf16[16,1152]{1,0:T(8,128)(2,1)S(1)}, u32[]{:S(2)}, u32[]{:S(2)}) collective-permute-start(bf16[16,1152]{1,0:T(8,128)(2,1)S(1)} %get-tuple-element.44), channel_id=1, source_target_pairs={{0,0},{1,4},{2,8},{3,12},{4,1},{5,5},{6,9},{7,13},{8,2},{9,6},{10,... | collective-permute-start | bytes 110600 | tf_op jit(solution)/shard_map/ppermute | solution.py:517
  30.2 8.7 %collective-permute-start.11 = (bf16[16,1152]{1,0:T(8,128)(2,1)S(1)}, bf16[16,1152]{1,0:T(8,128)(2,1)S(1)}, u32[]{:S(2)}, u32[]{:S(2)}) collective-permute-start(bf16[16,1152]{1,0:T(8,128)(2,1)S(1)} %get-tuple-element.44), channel_id=1, source_target_pairs={{0,2},{1,6},{2,10},{3,14},{4,3},{5,7},{6,11},{7,15},{8,0},{9,4},{1... | collective-permute-start | bytes 110600 | tf_op jit(solution)/shard_map/ppermute | solution.py:517
  33.0 6.7 %collective-permute-start.6 = (bf16[16,1152]{1,0:T(8,128)(2,1)S(1)}, bf16[16,1152]{1,0:T(8,128)(2,1)S(1)}, u32[]{:S(2)}, u32[]{:S(2)}) collective-permute-start(bf16[16,1152]{1,0:T(8,128)(2,1)S(1)} %get-tuple-element.43.refs_0_), channel_id=1, source_target_pairs={{0,4},{4,0},{8,12},{12,8},{1,5},{5,1},{9,13},{13,9},{2,6},{6,2},{1... | collective-permute-start | bytes 110600 | tf_op jit(solution)/shard_map/ppermute | solution.py:506
  34.6 5.2 %collective-permute-start.7 = (bf16[16,1152]{1,0:T(8,128)(2,1)S(1)}, bf16[16,1152]{1,0:T(8,128)(2,1)S(1)}, u32[]{:S(2)}, u32[]{:S(2)}) collective-permute-start(bf16[16,1152]{1,0:T(8,128)(2,1)S(1)} %get-tuple-element.43.refs_0_), channel_id=1, source_target_pairs={{0,8},{4,12},{8,0},{12,4},{1,9},{5,13},{9,1},{13,5},{2,10},{6,14},... | collective-permute-start | bytes 110600 | tf_op jit(solution)/shard_map/ppermute | solution.py:506
  35.5 5.8 %collective-permute-start.8 = (bf16[16,1152]{1,0:T(8,128)(2,1)S(1)}, bf16[16,1152]{1,0:T(8,128)(2,1)S(1)}, u32[]{:S(2)}, u32[]{:S(2)}) collective-permute-start(bf16[16,1152]{1,0:T(8,128)(2,1)S(1)} %get-tuple-element.43.refs_0_), channel_id=1, source_target_pairs={{0,12},{4,8},{8,4},{12,0},{1,13},{5,9},{9,5},{13,1},{2,14},{6,10},... | collective-permute-start | bytes 110600 | tf_op jit(solution)/shard_map/ppermute | solution.py:506
  37.4 3.9 %collective-permute-start.10 = (bf16[16,1152]{1,0:T(8,128)(2,1)S(1)}, bf16[16,1152]{1,0:T(8,128)(2,1)S(1)}, u32[]{:S(2)}, u32[]{:S(2)}) collective-permute-start(bf16[16,1152]{1,0:T(8,128)(2,1)S(1)} %collective-permute-done.9.refs_4_), channel_id=1, source_target_pairs={{0,1},{1,0},{2,3},{3,2},{4,5},{5,4},{6,7},{7,6},{8,9},{9,8},{10,11... | collective-permute-start | bytes 110600 | tf_op jit(solution)/shard_map/ppermute | solution.py:431
  38.9 2.4 %collective-permute-start.12 = (bf16[16,1152]{1,0:T(8,128)(2,1)S(1)}, bf16[16,1152]{1,0:T(8,128)(2,1)S(1)}, u32[]{:S(2)}, u32[]{:S(2)}) collective-permute-start(bf16[16,1152]{1,0:T(8,128)(2,1)S(1)} %collective-permute-done.11.refs_6_), channel_id=1, source_target_pairs={{0,1},{1,0},{2,3},{3,2},{4,5},{5,4},{6,7},{7,6},{8,9},{9,8},{10,11... | collective-permute-start | bytes 110600 | tf_op jit(solution)/shard_map/ppermute | solution.py:431
where the time goes:
time: 45.2 us; the launch traced here: 44.9 us
  starting transfers between devices  15.4 us (34%)
  Pallas kernels  14.5 us (32%)
  waiting for transfers between devices  14.3 us (32%)
  between operations  0.71 us (2%)
    pallas_call x6, Pallas kernels, run(): pl.pallas_call(body, out_shape=outs, in_specs=[pl.BlockSpec(memory_space=...  14.5 us
    ppermute x5, waiting for transfers between devices, shift(): lax.ppermute(value, axis, [(n, (n + step) % count) for n in range(count)])  6.49 us
    ppermute x3, waiting for transfers between devices, local(): lax.ppermute(bias_local, 'gx', [(n, n ^ m) for n in range(size_x)])  4.83 us
    ppermute x3, starting transfers between devices, local(): lax.ppermute(bias_local, 'gx', [(n, n ^ m) for n in range(size_x)])  4.48 us
    ppermute x3, starting transfers between devices, local(): lax.ppermute(left_own, 'gx', [(n, n ^ m) for n in range(size_x)])  4.39 us
    ppermute x2, starting transfers between devices, local(): got = lax.ppermute(right_own, ('gx', 'gy', 'gz'), pairs)  3.46 us
    ppermute x5, starting transfers between devices, shift(): lax.ppermute(value, axis, [(n, (n + step) % count) for n in range(count)])  3.04 us
    ppermute x3, waiting for transfers between devices, local(): lax.ppermute(left_own, 'gx', [(n, n ^ m) for n in range(size_x)])  1.52 us
  transfers between devices with their start and end apart: 13, of which 5 were waited for; matrix products, arithmetic and copies ran while one was open for 0% of the time, Pallas kernels for 8%

commit v1 on v0

v1 whole, which is shorter than its diff:
```python
import functools
import math

import jax
import jax.numpy as jnp
from jax import lax
from jax.experimental import pallas as pl
from jax.experimental.pallas import tpu as pltpu
from jax.sharding import PartitionSpec as P


LANES = 128
LAG = 4
SKEW = 4
SKEW_SMALL = 1
F32 = jnp.float32
BF16 = jnp.bfloat16


def iota(shape, dim):
    return lax.broadcasted_iota(jnp.int32, shape, dim)


def standardize(values):
    average = jnp.mean(values, axis=-1, keepdims=True)
    centred = values - average
    return centred * lax.rsqrt(jnp.mean(centred * centred, axis=-1, keepdims=True) + 1e-05)


def dot(left, right, contract=(1, 0), precision=None):
    return lax.dot_general(
        left,
        right,
        (((contract[0],), (contract[1],)), ((), ())),
        preferred_element_type=F32,
        precision=precision,
    )


def tiling_matrix(rows, columns):
    return (iota((rows, columns), 1) % rows == iota((rows, columns), 0)).astype(BF16)


def call(body, outs, scratch=(), flops=0, data=0, far=0, aliases={}):
    near = pl.BlockSpec(memory_space=pltpu.VMEM)
    held = sum(
        math.prod(ref.shape) * jnp.dtype(ref.dtype).itemsize
        for ref in scratch
        if hasattr(ref, "shape") and ref.memory_space == pltpu.VMEM
    )

    def run(*operands):
        operands = [
            pltpu.with_memory_space_constraint(x, pltpu.HBM) if n < far else x
            for n, x in enumerate(operands)
        ]
        return pl.pallas_call(
            body,
            out_shape=outs,
            in_specs=[pl.BlockSpec(memory_space=pltpu.HBM)] * far + [near] * (len(operands) - far),
            out_specs=jax.tree.map(lambda _: near, outs),
            scratch_shapes=scratch,
            cost_estimate=pl.CostEstimate(flops=flops, bytes_accessed=data, transcendentals=0),
            compiler_params=pltpu.CompilerParams(vmem_limit_bytes=held * 5 // 4 + (6 << 20)),
            input_output_aliases=aliases,
        )(*operands)

    return run


def fetch(sources, targets, sems):
    copies = [
        pltpu.make_async_copy(source, target, sems.at[n])
        for n, (source, target) in enumerate(zip(sources, targets))
    ]
    for copy in copies:
        copy.start()
    return copies


def embed_kernel(
    ids_far,
    mask_far,
    profile_far,
    table_far,
    pair_far,
    matrix_far,
    msg_ref,
    arriving_ref,
    mask_ref,
    pair_ref,
    matrix_ref,
    ids_ref,
    profile_ref,
    table_ref,
    padded,
    sems,
):
    copies = fetch(
        (ids_far, table_far, mask_far, profile_far, pair_far, matrix_far),
        (ids_ref, table_ref, mask_ref, profile_ref, pair_ref, matrix_ref),
        sems,
    )
    sequences, residues, features = profile_ref.shape
    kinds = table_ref.shape[0]
    for copy in copies[:3]:
        copy.wait()
    padded[...] = jnp.zeros_like(padded)
    padded[0:kinds, :] = table_ref[...]
    columns = ids_ref[...].astype(F32).T
    labels = iota((residues, padded.shape[0]), 1).astype(F32)
    rows = sequences * residues
    mask = mask_ref[...].astype(F32).astype(BF16)
    msg_ref[rows:, :] = dot(mask, tiling_matrix(residues, features)).astype(BF16)
    table = padded[...]
    copies[3].wait()
    step = 4
    for start in range(0, sequences, step):
        hot = [
            (columns[:, s : s + 1] == labels).astype(F32).astype(BF16)
            for s in range(start, start + step)
        ]
        where = slice(start * residues, (start + step) * residues)
        profile = profile_ref[start : start + step].reshape(step * residues, features)
        arriving = profile.astype(F32) + dot(jnp.concatenate(hot, axis=0), table)
        arriving_ref[where, :] = arriving
        msg_ref[where, :] = standardize(arriving).astype(BF16)
    for copy in copies[4:]:
        copy.wait()


def prepare_kernel(weights, *refs):
    far, (pair_ref, matrix_ref), refs = refs[:weights], refs[weights : weights + 2], refs[weights + 2 :]
    near, (out_ref, sems) = refs[:weights], refs[weights:]
    copies = fetch(far, near, sems)
    rows, columns, width = pair_ref.shape
    matrix = matrix_ref[...]
    step = LANES // columns
    for start in range(0, rows, step):
        part = pair_ref[start : start + step].reshape(step * columns, width).astype(F32)
        bias = dot(matrix, standardize(part), (1, 1), lax.Precision.HIGHEST)
        out_ref[:, start * columns : (start + step) * columns] = bias
    for copy in copies:
        copy.wait()


def block_kernel(mix_ref, block_ref, wide):
    turns = block_ref.shape[0]
    width = other = math.isqrt(mix_ref.shape[0])
    pitch = wide.shape[0] // width
    for c in range(width):
        wide[c * pitch : c * pitch + other, :] = mix_ref[c * other : (c + 1) * other, :].astype(F32)
    for d in range(other):
        piece = wide[pl.ds(d, width, stride=pitch), :].astype(BF16)
        high, low = divmod(d, turns)
        for turn in range(turns):
            spot = (high * turns + (low + turn) % turns) * width
            block_ref[turn, spot : spot + width, :] = piece


def block_rows(shift, residues):
    shift_y, shift_z, size_y, size_z = shift
    block = lax.rem(lax.axis_index("gy") - shift_y + size_y, size_y) * size_z + lax.rem(
        lax.axis_index("gz") - shift_z + size_z, size_z
    )
    return block, pl.ds(pl.multiple_of(block * residues, residues), residues)


def project_kernel(position, *refs):
    msgs = refs[: len(position)]
    wq_ref, wk_ref, wv_ref, wg_ref, q_ref, k_ref, v_ref, g_ref = refs[len(position) :]
    sequences, residues, _ = q_ref.shape
    rows = sequences * residues
    for msg, place in zip(msgs, position):
        _, where = block_rows(place, residues)
        normed = msg[0:rows, :]
        k_ref[:, where, :] = dot(normed, wk_ref[...]).astype(BF16).reshape(q_ref.shape)
        v_ref[:, where, :] = dot(normed, wv_ref[...]).astype(BF16).reshape(q_ref.shape)
    own = msgs[0][0:rows, :]
    q_ref[...] = dot(own, wq_ref[...]).astype(BF16).reshape(q_ref.shape)
    g_ref[...] = jax.nn.sigmoid(dot(own, wg_ref[...])).reshape(g_ref.shape)


def score_kernel(heads, position, late, *refs):
    msgs = refs[: len(position)]
    q_ref, _, _, wk_ref, wv_ref, k_ref, v_ref, scored, pen_ref = refs[len(position) :]
    sequences, residues, features = q_ref.shape
    rows = sequences * residues
    total = pen_ref.shape[1]
    lane_block = iota((sequences, total), 1) // residues
    present = jnp.zeros((sequences, total), F32)
    for n, (msg, place) in enumerate(zip(msgs, position)):
        block, where = block_rows(place, residues)
        if n in late:
            normed = msg[0:rows, :]
            k_ref[:, where, :] = dot(normed, wk_ref[...]).astype(BF16).reshape(q_ref.shape)
            v_ref[:, where, :] = dot(normed, wv_ref[...]).astype(BF16).reshape(q_ref.shape)
        tiled = msg[rows : rows + sequences, :].astype(F32)
        while tiled.shape[1] < total:
            tiled = jnp.concatenate([tiled, tiled], axis=1)
        present = jnp.where(lane_block == block, tiled[:, 0:total], present)
    pen_ref[...] = (present - 1.0) * 1000000000.0
    size = features // heads
    per = LANES // size
    span = per * residues
    scale = size ** (-0.5)
    own_lanes = iota((span, LANES), 0) // residues == iota((span, LANES), 1) // size
    for s in range(sequences):
        for part in range(heads // per):
            lanes = slice(part * LANES, (part + 1) * LANES)
            stacked = jnp.concatenate([q_ref[s, :, lanes]] * per, axis=0)
            stacked = jnp.where(own_lanes, stacked, jnp.zeros_like(stacked))
            scored[s, part * span : (part + 1) * span, :] = (
                dot(stacked, k_ref[s, :, lanes], (1, 1)) * scale
            )


def attend_kernel(heads, groups, *refs):
    attend_body(heads, refs[:groups], *refs[groups:])


def attend_body(
    heads,
    biases,
    scored,
    v_ref,
    g_ref,
    pen_ref,
    arriving_ref,
    mask_ref,
    wr_ref,
    wf_ref,
    ws_ref,
    profile_ref,
    left_ref,
    right_ref,
    bias_ref,
    spread,
    bias,
    weighed,
    gated,
    leftish,
    rightish,
):
    sequences, residues, features = g_ref.shape
    total = v_ref.shape[1]
    size = features // heads
    per = LANES // size
    fit = LANES // residues
    pitch = spread.shape[1] // residues
    z_own = lax.axis_index("gx")
    for other, ref in enumerate(biases):
        bias_ref[z_own ^ other] = ref[...]
    lane = iota((heads, LANES), 1) // residues
    for i in range(residues):
        tile, inner = divmod(i, fit)
        for column in range(total // LANES):
            value = None
            for slot in range(fit):
                source = bias_ref[
                    column * fit + slot, :, tile * LANES : (tile + 1) * LANES
                ]
                shift = ((slot - inner) % fit) * residues
                if shift:
                    source = pltpu.roll(source, shift, 1)
                value = source if value is None else jnp.where(lane == slot, source, value)
            spread[column, i * pitch : i * pitch + heads, :] = value
    for column in range(total // LANES):
        for h in range(heads):
            bias[
                h * residues : (h + 1) * residues, column * LANES : (column + 1) * LANES
            ] = spread[column, pl.ds(h, residues, stride=pitch), :]
    span = per * residues
    small_lanes = [iota((residues, LANES), 1) // size == p for p in range(per)]
    parts = [
        (slice(part * LANES, (part + 1) * LANES), slice(part * span, (part + 1) * span))
        for part in range(heads // per)
    ]
    ones = jnp.ones((total, LANES), BF16)

    def weigh(s):
        penalty = pen_ref[s : s + 1, :]
        for lanes, span_rows in parts:
            scores = scored[s, span_rows, :] + bias[span_rows, :] + penalty
            top = jnp.max(scores, axis=1, keepdims=True)
            weighed[s, span_rows, :] = jnp.exp(scores - top).astype(BF16)

    def gather(s):
        for lanes, span_rows in parts:
            mixed = dot(
                weighed[s, span_rows, :], jnp.concatenate([v_ref[s, :, lanes], ones], axis=1)
            )
            value = mixed[0:residues, :]
            for p in range(1, per):
                rows = slice(p * residues, (p + 1) * residues)
                mask = jnp.concatenate([small_lanes[p], small_lanes[p]], axis=1)
                value = jnp.where(mask, mixed[rows, :], value)
            gated[s, :, lanes] = (
                g_ref[s, :, lanes] * (value[:, :LANES] / value[:, LANES:])
            ).astype(BF16)

    for step in range(sequences + LAG):
        if step < sequences:
            weigh(step)
        if step >= LAG:
            gather(step - LAG)

    rows = sequences * residues
    refreshed = (
        arriving_ref[...] + dot(gated[...].reshape(rows, features), wr_ref[...])
    ).astype(BF16)
    profile_ref[...] = refreshed.reshape(profile_ref.shape)
    normed = standardize(refreshed.astype(F32)).astype(BF16)
    width = ws_ref.shape[0]
    left_pitch, right_pitch = leftish.shape[0] // sequences, rightish.shape[0] // sequences
    sides = dot(normed, jnp.concatenate([wf_ref[...]] * (LANES // width)), (1, 1))
    for s in range(sequences):
        piece = normed[s * residues : (s + 1) * residues, :]
        leftish[s * left_pitch : s * left_pitch + residues, :] = sides[
            s * residues : (s + 1) * residues, :
        ]
        rightish[s * right_pitch : s * right_pitch + width, :] = dot(
            ws_ref[...], jnp.concatenate([piece] * fit, axis=0), (1, 1)
        )
    mask = mask_ref[...].astype(F32).astype(BF16)
    wide = residues * width
    expand = (iota((residues, wide), 1) // width == iota((residues, wide), 0)).astype(BF16)
    left_mask = dot(mask, expand)
    right_mask = dot(mask, tiling_matrix(residues, LANES))
    turns = LANES // width
    high = width // turns
    left_order = list(range(residues))
    right_order = [h * turns + low for low in range(turns) for h in range(high)]
    for tile in range(wide // LANES):
        lanes = slice(tile * LANES, (tile + 1) * LANES)
        for source, pitch, step, order, target, present in (
            (leftish, left_pitch, width, left_order, left_ref, left_mask[:, lanes]),
            (rightish, right_pitch, residues, right_order, right_ref, right_mask),
        ):
            group = iota((sequences, LANES), 1) // step
            count = LANES // step
            value = None
            for p in range(count):
                other = source[pl.ds(order[tile * count + p], sequences, stride=pitch), :]
                value = other if p == 0 else jnp.where(group == p, other, value)
            target[:, lanes] = (value * present).astype(BF16)
    left_ref[:, wide:] = right_mask.astype(BF16)
    right_ref[:, wide:] = right_mask.astype(BF16)


def pair_kernel(left_from, right_from, *refs):
    lefts = refs[: len(left_from)]
    rights = refs[len(left_from) : len(left_from) + len(right_from)]
    (pair_ref, block_ref, w1_ref, w2_ref, out_ref, left, right, flipped, spread, stacked, middle, normed) = refs[
        len(left_from) + len(right_from) :
    ]
    sequences = lefts[0].shape[0]
    rows, columns, _ = pair_ref.shape
    z_own, x_own, c_own = (lax.axis_index(n) for n in ("gx", "gy", "gz"))
    for ref, other in zip(lefts, left_from):
        start = (z_own ^ other) * sequences
        left[pl.ds(pl.multiple_of(start, sequences), sequences), :] = ref[...]
    for ref, (shift_y, shift_z, size_y, size_z) in zip(rights, right_from):
        block = lax.rem(x_own - shift_y + size_y, size_y) * size_z + lax.rem(
            c_own - shift_z + size_z, size_z
        )
        right[pl.ds(pl.multiple_of(block * sequences, sequences), sequences), :] = ref[...]
    wide = left.shape[1] - LANES
    width = wide // rows
    fit = LANES // width
    high = wide // columns // fit
    count = dot(right[:, wide:], left[:, wide:], (0, 0))[0:columns, :]
    share = 1.0 / (count + 1.0)
    tiles = wide // LANES
    deep = left.shape[0]
    span = high * columns
    flipped[...] = jnp.concatenate(
        [right[:, low * span : (low + 1) * span] for low in range(fit)]
    ).T
    group = iota((deep, LANES), 1) // width
    for tile in range(tiles):
        lanes = slice(tile * LANES, (tile + 1) * LANES)
        chunk = left[:, lanes].astype(F32)
        for low in range(fit):
            rolled = pltpu.roll(chunk, low * width, 1) if low else chunk
            for turn in range(fit):
                spread[turn, low * deep : (low + 1) * deep, lanes] = jnp.where(
                    group == (low + turn) % fit, rolled, 0.0
                ).astype(BF16)

    def outer(turn):
        value = dot(flipped[...], spread[turn]).astype(BF16)
        for tile in range(tiles):
            for h in range(high):
                stacked[
                    turn, tile * columns : (tile + 1) * columns, h * LANES : (h + 1) * LANES
                ] = value[h * columns : (h + 1) * columns, tile * LANES : (tile + 1) * LANES]

    def mix(turn):
        mixed = dot(stacked[turn], block_ref[turn])
        for tile in range(tiles):
            i = tile * fit + turn
            where = slice(tile * columns, (tile + 1) * columns)
            middle[turn, where, :] = pair_ref[i].astype(F32) + mixed[where, :] * share[:, i : i + 1]

    def norm(turn):
        normed[turn] = standardize(middle[turn]).astype(BF16)

    def transition(turn):
        hidden = jnp.maximum(dot(normed[turn], w1_ref[...]), 0.0).astype(BF16)
        done = (middle[turn] + dot(hidden, w2_ref[...])).astype(BF16)
        for tile in range(tiles):
            out_ref[tile * fit + turn] = done[tile * columns : (tile + 1) * columns, :]

    stages = (outer, mix, norm, transition)
    for step in range(fit + len(stages) - 1):
        for late, stage in reversed(list(enumerate(stages))):
            if 0 <= step - late < fit:
                stage(step - late)


def local(
    sizes,
    alignment_token_ids,
    homolog_profile,
    alignment_mask,
    pair_features,
    symbol_lookup_weights,
    asking_weights,
    lookup_weights,
    content_weights,
    sigmoid_switch_weights,
    resulting_weights,
    pair_bias_matrix,
    first_factor_weights,
    second_factor_weights,
    outer_mixing_weight,
    widening_weight,
    narrowing_weight,
):
    size_x, size_y, size_z = sizes
    sequences, residues, features = homolog_profile.shape
    heads = pair_bias_matrix.shape[1]
    width = first_factor_weights.shape[1]
    pair_rows, pair_columns, pair_width = pair_features.shape
    total = residues * size_y * size_z
    rows = sequences * residues
    shape = jax.ShapeDtypeStruct

    local_pair = shape(pair_features.shape, BF16)
    local_mask = shape(alignment_mask.shape, jnp.int32)
    matrix_far = pair_bias_matrix.T
    msg, arriving, mask, pair, matrix = call(
        embed_kernel,
        (
            shape((rows + sequences, features), BF16),
            shape((rows, features), F32),
            local_mask,
            local_pair,
            shape(matrix_far.shape, F32),
        ),
        [
            pltpu.VMEM(alignment_token_ids.shape, jnp.int32),
            pltpu.VMEM(homolog_profile.shape, BF16),
            pltpu.VMEM(symbol_lookup_weights.shape, BF16),
            pltpu.VMEM((LANES, features), BF16),
            pltpu.SemaphoreType.DMA((6,)),
        ],
        flops=2 * rows * LANES * features,
        data=rows * features * 8,
        far=6,
    )(
        alignment_token_ids,
        alignment_mask,
        homolog_profile,
        symbol_lookup_weights,
        pair_features,
        matrix_far,
    )

    def shift(value, axis, count, step):
        return lax.ppermute(value, axis, [(n, (n + step) % count) for n in range(count)])

    far = [msg] + [shift(msg, "gy", size_y, r) for r in range(1, size_y)]
    position, msgs = [], []
    for r in range(size_y):
        for t in range(size_z):
            position.append((r, t, size_y, size_z))
            msgs.append(far[r] if t == 0 else shift(far[r], "gz", size_z, t))

    fit = LANES // width
    weights = (
        asking_weights,
        lookup_weights,
        content_weights,
        sigmoid_switch_weights,
        resulting_weights,
        first_factor_weights.T,
        second_factor_weights.T,
        widening_weight,
        narrowing_weight,
        outer_mixing_weight,
    )
    wq, wk, wv, wg, wr, wf, ws, w1, w2, mix, bias_local = call(
        functools.partial(prepare_kernel, len(weights)),
        tuple(shape(w.shape, w.dtype) for w in weights)
        + (shape((heads, pair_rows * pair_columns), F32),),
        [pltpu.SemaphoreType.DMA((len(weights),))],
        flops=2 * 6 * pair_rows * pair_columns * pair_width * LANES,
        data=pair_rows * pair_columns * pair_width * 2,
        far=len(weights),
    )(*weights, pair, matrix)
    biases = [bias_local]
    for m in range(1, size_x):
        biases.append(lax.ppermute(bias_local, "gx", [(n, n ^ m) for n in range(size_x)]))

    three = (sequences, residues, features)
    keys = (sequences, total, features)
    scores = (sequences, heads * residues, total)
    late = tuple(n for n, (r, t, _, _) in enumerate(position) if r and t)
    early = tuple(n for n in range(len(position)) if n not in late)
    queries, keys_early, values_early, gates = call(
        functools.partial(project_kernel, tuple(position[n] for n in early)),
        (shape(three, BF16), shape(keys, BF16), shape(keys, BF16), shape(three, F32)),
        flops=2 * rows * features * features * 2 * (len(early) + 1),
        data=sequences * total * features * 6,
    )(*(msgs[n] for n in early), wq, wk, wv, wg)
    _, values, scored, penalty = call(
        functools.partial(score_kernel, heads, tuple(position), late),
        (
            shape(keys, BF16),
            shape(keys, BF16),
            shape(scores, F32),
            shape((sequences, total), F32),
        ),
        flops=2 * rows * features * features * 2 * len(late),
        data=sequences * total * features * 6,
        aliases={len(msgs) + 1: 0, len(msgs) + 2: 1},
    )(*msgs, queries, keys_early, values_early, wk, wv)

    wide = residues * width
    message = shape((sequences, wide + LANES), BF16)
    refreshed, left_own, right_own = call(
        functools.partial(attend_kernel, heads, size_x),
        (shape(three, BF16), message, message),
        [
            pltpu.VMEM((size_x, heads, pair_rows * pair_columns), F32),
            pltpu.VMEM((total // LANES, residues * (heads + SKEW_SMALL), LANES), F32),
            pltpu.VMEM(scores[1:], F32),
            pltpu.VMEM(scores, BF16),
            pltpu.VMEM(three, BF16),
            pltpu.VMEM((sequences * (residues + SKEW), LANES), F32),
            pltpu.VMEM((sequences * (width + SKEW), LANES), F32),
        ],
        flops=4 * sequences * heads * residues * total * LANES,
        data=sequences * total * features * 4,
    )(*biases, scored, values, gates, penalty, arriving, mask, wr, wf, ws)

    lefts = [left_own]
    for m in range(1, size_x):
        lefts.append(lax.ppermute(left_own, "gx", [(n, n ^ m) for n in range(size_x)]))
    right_from, rights = [], []
    blocks = size_y * size_z
    for r in range(size_y):
        pairs = []
        for a in range(size_x):
            for b in range(blocks):
                to = ((a // size_z + r) % size_y) * size_z + a % size_z
                pairs.append((a * blocks + b, b * blocks + to))
        got = lax.ppermute(right_own, ("gx", "gy", "gz"), pairs)
        for t in range(size_z):
            right_from.append((r, t, size_y, size_z))
            rights.append(got if t == 0 else shift(got, "gz", size_z, t))

    block = call(
        block_kernel,
        shape((fit, width * width, pair_width), BF16),
        [pltpu.VMEM((width * (width + SKEW), pair_width), F32)],
        data=width * width * fit * pair_width * 2,
    )(mix)

    depth = sequences * size_x
    pair_output = call(
        functools.partial(pair_kernel, tuple(range(size_x)), tuple(right_from)),
        shape(pair_features.shape, BF16),
        [
            pltpu.VMEM((depth, wide + LANES), BF16),
            pltpu.VMEM((depth, wide + LANES), BF16),
            pltpu.VMEM((width // fit * pair_columns, fit * depth), BF16),
            pltpu.VMEM((fit, fit * depth, wide), BF16),
            pltpu.VMEM((fit, pair_rows // fit * pair_columns, width * width), BF16),
            pltpu.VMEM((fit, pair_rows // fit * pair_columns, pair_width), F32),
            pltpu.VMEM((fit, pair_rows // fit * pair_columns, pair_width), BF16),
        ],
        flops=2 * pair_rows * pair_columns * width * width * pair_width * fit,
        data=width * width * fit * pair_width * fit * 2,
    )(*lefts, *rights, pair, block, w1, w2)
    return refreshed, pair_output


def solution(mesh):
    sizes = tuple(mesh.shape[name] for name in ("gx", "gy", "gz"))
    assert sizes[0] == sizes[1] * sizes[2] and sizes[0] & (sizes[0] - 1) == 0
    in_specs = (
        P(("grp", "gx"), ("gy", "gz")),
        P(("grp", "gx"), ("gy", "gz"), None),
        P(("grp", "gx"), ("gy", "gz")),
        P(("grp", "gy", "gz"), "gx", None),
    ) + (P(),) * 12
    out_specs = (P(("grp", "gx"), ("gy", "gz"), None), P(("grp", "gy", "gz"), "gx", None))

    def body(*args):
        return local(sizes, *args)

    return jax.shard_map(
        body, mesh=mesh, in_specs=in_specs, out_specs=out_specs, check_vma=False
    )
```

time: 45.2 us -> 41.2 us (0.912)
  Pallas kernels: 14.5 us -> 10.8 us
    pallas_call x6 -> x7, Pallas kernels: 14.5 us -> 10.8 us  [run(): pl.pallas_call(body, out_shape=outs, in_specs=[pl.BlockSpec(memory_space=...]
    ppermute x3, waiting for transfers between devices: 4.83 us -> 3.89 us  [local(): lax.ppermute(bias_local, 'gx', [(n, n ^ m) for n in range(size_x)])]
    ppermute x3, waiting for transfers between devices: 1.52 us -> 2.14 us  [local(): lax.ppermute(left_own, 'gx', [(n, n ^ m) for n in range(size_x)])]
  transfers between devices with their start and end apart: 13 -> 13, of which waited for: 5 -> 6; matrix products, arithmetic and copies ran while one was open for 0% -> 0% of each run, Pallas kernels for 8% -> 9%
where the time goes in v1:
time: 41.2 us; the launch traced here: 41 us
  starting transfers between devices  15.4 us (37%)
  waiting for transfers between devices  14.1 us (34%)
  Pallas kernels  10.8 us (26%)
  between operations  0.7 us (2%)
    pallas_call x7, Pallas kernels, run(): pl.pallas_call(body, out_shape=outs, in_specs=[pl.BlockSpec(memory_space=...  10.8 us
    ppermute x5, waiting for transfers between devices, shift(): lax.ppermute(value, axis, [(n, (n + step) % count) for n in range(count)])  6.49 us
    ppermute x3, starting transfers between devices, local(): lax.ppermute(bias_local, 'gx', [(n, n ^ m) for n in range(size_x)])  4.48 us
    ppermute x3, starting transfers between devices, local(): lax.ppermute(left_own, 'gx', [(n, n ^ m) for n in range(size_x)])  4.39 us
    ppermute x3, waiting for transfers between devices, local(): lax.ppermute(bias_local, 'gx', [(n, n ^ m) for n in range(size_x)])  3.89 us
    ppermute x2, starting transfers between devices, local(): got = lax.ppermute(right_own, ('gx', 'gy', 'gz'), pairs)  3.45 us
    ppermute x5, starting transfers between devices, shift(): lax.ppermute(value, axis, [(n, (n + step) % count) for n in range(count)])  3.04 us
    ppermute x3, waiting for transfers between devices, local(): lax.ppermute(left_own, 'gx', [(n, n ^ m) for n in range(size_x)])  2.14 us
  transfers between devices with their start and end apart: 13, of which 6 were waited for; matrix products, arithmetic and copies ran while one was open for 0% of the time, Pallas kernels for 9%

profile of v1, /device:TPU:0, one launch (start us, length us, event | category | flops | bytes accessed | tf_op | source)
XLA Modules:
  0.0 41.0 jit_solution(12343341500018006141)
XLA Ops:
  0.6 1.5 %shard_map.167 = (bf16[528,256]{1,0:T(8,128)(2,1)S(1)}, f32[512,256]{1,0:T(8,128)S(1)}, s32[16,32]{1,0:T(8,128)S(1)}, bf16[32,32,128]{2,1,0:T(8,128)(2,1)S(1)}, f32[8,128]{1,0:T(8,128)S(1)}) custom-call(s32[16,32]{1,0:T(8,128)} %ids_far.1, s32[16,32]{1,0:T(8,128)} %mask_far.1, bf16[16,32,256]{2,1,0:T(8,128)(2,1)} %profile_far.1, bf16[23,256]{1,0:T(8,128)(2,1)} %table_far.1, ...), custom_call_target="tpu_custom_call" | custom-call | flops 33554432 | bytes 1048576 | tf_op jit(solution)/shard_map/pallas_call | solution.py:57
  2.2 3.0 %collective-permute-start.4 = (bf16[528,256]{1,0:T(8,128)(2,1)S(1)}, bf16[528,256]{1,0:T(8,128)(2,1)S(1)}, u32[]{:S(2)}, u32[]{:S(2)}) collective-permute-start(bf16[528,256]{1,0:T(8,128)(2,1)S(1)} %get-tuple-element.31.refs_0_), channel_id=1, source_target_pairs={{0,2},{2,0},{1,3},{3,1},{4,6},{6,4},{5,7},{7,5},{8,10},{10,8},{9,1... | collective-permute-start | bytes 811016 | tf_op jit(solution)/shard_map/ppermute | solution.py:482
  5.2 0.0 collective-permute-start.3
  5.2 6.5 %collective-permute-done.4.refs_2_ = bf16[528,256]{1,0:T(8,128)(2,1)S(1)} collective-permute-done((bf16[528,256]{1,0:T(8,128)(2,1)S(1)}, bf16[528,256]{1,0:T(8,128)(2,1)S(1)}, u32[]{:S(2)}, u32[]{:S(2)}) %collective-permute-start.4) | collective-permute-done | bytes 270368 | tf_op jit(solution)/shard_map/ppermute | solution.py:482
  11.7 0.0 collective-permute-start.5
  11.7 1.9 %shard_map.168 = (bf16[256,256]{1,0:T(8,128)(2,1)S(1)}, bf16[256,256]{1,0:T(8,128)(2,1)S(1)}, bf16[256,256]{1,0:T(8,128)(2,1)S(1)}, bf16[256,256]{1,0:T(8,128)(2...) custom-call(bf16[256,256]{1,0:T(8,128)(2,1)} %refs_0_.1, ...), custom_call_target="tpu_custom_call" | custom-call | flops 201326592 | bytes 262144 | tf_op jit(solution)/shard_map/pallas_call | solution.py:57
  13.6 1.9 %collective-permute-start = (f32[8,1024]{1,0:T(8,128)S(1)}, f32[8,1024]{1,0:T(8,128)S(1)}, u32[]{:S(2)}, u32[]{:S(2)}) collective-permute-start(f32[8,1024]{1,0:T(8,128)S(1)} %get-tuple-element.30.refs_0_), channel_id=1, source_target_pairs={{0,4},{4,0},{8,12},{12,8},{1,5},{5,1},{9,13},{13,9},{2,6},{6,2},{1... | collective-permute-start | bytes 98312 | tf_op jit(solution)/shard_map/ppermute | solution.py:515
  15.5 2.6 %collective-permute-start.1 = (f32[8,1024]{1,0:T(8,128)S(1)}, f32[8,1024]{1,0:T(8,128)S(1)}, u32[]{:S(2)}, u32[]{:S(2)}) collective-permute-start(f32[8,1024]{1,0:T(8,128)S(1)} %get-tuple-element.30.refs_0_), channel_id=1, source_target_pairs={{0,8},{4,12},{8,0},{12,4},{1,9},{5,13},{9,1},{13,5},{2,10},{6,14},... | collective-permute-start | bytes 98312 | tf_op jit(solution)/shard_map/ppermute | solution.py:515
  18.1 0.0 collective-permute-start.2
  18.1 0.0 collective-permute-done.3.refs_1_
  18.1 0.7 %shard_map.169 = (bf16[16,32,256]{2,1,0:T(8,128)(2,1)S(1)}, bf16[16,128,256]{2,1,0:T(8,128)(2,1)S(1)}, bf16[16,128,256]{2,1,0:T(8,128)(2,1)S(1)}, f32[16,32,256]{2,1,0:T(8,128)S(1)}) custom-call(bf16[528,256]{1,0:T(8,128)(2,1)S(1)} %get-tuple-element.31.refs_0_, bf16[528,256]{1,0:T(8,128)(2,1)S(1)} %collective-permute-done.3.refs_1_, ...), custom_call_target="tpu_custom_call" | custom-call | flops 536870912 | bytes 3145728 | tf_op jit(solution)/shard_map/pallas_call | solution.py:57
  18.8 0.0 collective-permute-done.5.refs_3_
  18.8 1.1 %shard_map.170 = (bf16[16,128,256]{2,1,0:T(8,128)(2,1)S(1)}, bf16[16,128,256]{2,1,0:T(8,128)(2,1)S(1)}, f32[16,256,128]{2,1,0:T(8,128)S(1)}, f32[16,128]{1,0:T(8,128)S(1)}) custom-call(bf16[528,256]{1,0:T(8,128)(2,1)S(1)} %get-tuple-element.31.refs_0_, ...), custom_call_target="tpu_custom_call", output_to_operand_aliasing={{0}: (5, {}), {1}: (6, {})} | custom-call | flops 134217728 | bytes 3145728 | tf_op jit(solution)/shard_map/pallas_call | solution.py:57
  19.9 0.0 collective-permute-done.refs_1_
  19.9 0.9 %collective-permute-done.1.refs_2_ = f32[8,1024]{1,0:T(8,128)S(1)} collective-permute-done((f32[8,1024]{1,0:T(8,128)S(1)}, f32[8,1024]{1,0:T(8,128)S(1)}, u32[]{:S(2)}, u32[]{:S(2)}) %collective-permute-start.1) | collective-permute-done | bytes 32800 | tf_op jit(solution)/shard_map/ppermute | solution.py:515
  20.8 3.0 %collective-permute-done.2.refs_3_ = f32[8,1024]{1,0:T(8,128)S(1)} collective-permute-done((f32[8,1024]{1,0:T(8,128)S(1)}, f32[8,1024]{1,0:T(8,128)S(1)}, u32[]{:S(2)}, u32[]{:S(2)}) %collective-permute-start.2) | collective-permute-done | bytes 32800 | tf_op jit(solution)/shard_map/ppermute | solution.py:515
  23.8 2.1 %shard_map.171 = (bf16[16,32,256]{2,1,0:T(8,128)(2,1)}, bf16[16,1152]{1,0:T(8,128)(2,1)S(1)}, bf16[16,1152]{1,0:T(8,128)(2,1)S(1)}) custom-call(f32[8,1024]{1,0:T(8,128)S(1)} %get-tuple-element.30.refs_0_, f32[8,1024]{1,0:T(8,128)S(1)} %collective-permute-done.refs_1_, f32[8,1024]{1,0:T(8,128)S(1)} %collective-permute-done.1.refs_2_, ...), custom_call_target="tpu_custom_call" | custom-call | flops 268435456 | bytes 2097152 | tf_op jit(solution)/shard_map/pallas_call | solution.py:57
  25.8 0.7 %collective-permute-start.9 = (bf16[16,1152]{1,0:T(8,128)(2,1)S(1)}, bf16[16,1152]{1,0:T(8,128)(2,1)S(1)}, u32[]{:S(2)}, u32[]{:S(2)}) collective-permute-start(bf16[16,1152]{1,0:T(8,128)(2,1)S(1)} %get-tuple-element.50), channel_id=1, source_target_pairs={{0,0},{1,4},{2,8},{3,12},{4,1},{5,5},{6,9},{7,13},{8,2},{9,6},{10,... | collective-permute-start | bytes 110600 | tf_op jit(solution)/shard_map/ppermute | solution.py:570
  26.5 2.8 %collective-permute-start.11 = (bf16[16,1152]{1,0:T(8,128)(2,1)S(1)}, bf16[16,1152]{1,0:T(8,128)(2,1)S(1)}, u32[]{:S(2)}, u32[]{:S(2)}) collective-permute-start(bf16[16,1152]{1,0:T(8,128)(2,1)S(1)} %get-tuple-element.50), channel_id=1, source_target_pairs={{0,2},{1,6},{2,10},{3,14},{4,3},{5,7},{6,11},{7,15},{8,0},{9,4},{1... | collective-permute-start | bytes 110600 | tf_op jit(solution)/shard_map/ppermute | solution.py:570
  29.3 1.6 %collective-permute-start.6 = (bf16[16,1152]{1,0:T(8,128)(2,1)S(1)}, bf16[16,1152]{1,0:T(8,128)(2,1)S(1)}, u32[]{:S(2)}, u32[]{:S(2)}) collective-permute-start(bf16[16,1152]{1,0:T(8,128)(2,1)S(1)} %get-tuple-element.49.refs_0_), channel_id=1, source_target_pairs={{0,4},{4,0},{8,12},{12,8},{1,5},{5,1},{9,13},{13,9},{2,6},{6,2},{1... | collective-permute-start | bytes 110600 | tf_op jit(solution)/shard_map/ppermute | solution.py:561
  30.9 1.0 %collective-permute-start.7 = (bf16[16,1152]{1,0:T(8,128)(2,1)S(1)}, bf16[16,1152]{1,0:T(8,128)(2,1)S(1)}, u32[]{:S(2)}, u32[]{:S(2)}) collective-permute-start(bf16[16,1152]{1,0:T(8,128)(2,1)S(1)} %get-tuple-element.49.refs_0_), channel_id=1, source_target_pairs={{0,8},{4,12},{8,0},{12,4},{1,9},{5,13},{9,1},{13,5},{2,10},{6,14},... | collective-permute-start | bytes 110600 | tf_op jit(solution)/shard_map/ppermute | solution.py:561
  31.8 1.9 %collective-permute-start.8 = (bf16[16,1152]{1,0:T(8,128)(2,1)S(1)}, bf16[16,1152]{1,0:T(8,128)(2,1)S(1)}, u32[]{:S(2)}, u32[]{:S(2)}) collective-permute-start(bf16[16,1152]{1,0:T(8,128)(2,1)S(1)} %get-tuple-element.49.refs_0_), channel_id=1, source_target_pairs={{0,12},{4,8},{8,4},{12,0},{1,13},{5,9},{9,5},{13,1},{2,14},{6,10},... | collective-permute-start | bytes 110600 | tf_op jit(solution)/shard_map/ppermute | solution.py:561
  33.7 0.0 collective-permute-done.9.refs_4_
  33.7 1.6 %collective-permute-done.11.refs_6_ = bf16[16,1152]{1,0:T(8,128)(2,1)S(1)} collective-permute-done((bf16[16,1152]{1,0:T(8,128)(2,1)S(1)}, bf16[16,1152]{1,0:T(8,128)(2,1)S(1)}, u32[]{:S(2)}, u32[]{:S(2)}) %collective-permute-start.11) | collective-permute-done | bytes 36896 | tf_op jit(solution)/shard_map/ppermute | solution.py:570
  35.3 0.0 collective-permute-start.12
  35.3 0.1 shard_map.172.refs_9_
  35.4 0.0 collective-permute-done.6.refs_1_
  35.4 0.6 %collective-permute-done.7.refs_2_ = bf16[16,1152]{1,0:T(8,128)(2,1)S(1)} collective-permute-done((bf16[16,1152]{1,0:T(8,128)(2,1)S(1)}, bf16[16,1152]{1,0:T(8,128)(2,1)S(1)}, u32[]{:S(2)}, u32[]{:S(2)}) %collective-permute-start.7) | collective-permute-done | bytes 36896 | tf_op jit(solution)/shard_map/ppermute | solution.py:561
  36.1 1.5 %collective-permute-done.8.refs_3_ = bf16[16,1152]{1,0:T(8,128)(2,1)S(1)} collective-permute-done((bf16[16,1152]{1,0:T(8,128)(2,1)S(1)}, bf16[16,1152]{1,0:T(8,128)(2,1)S(1)}, u32[]{:S(2)}, u32[]{:S(2)}) %collective-permute-start.8) | collective-permute-done | bytes 36896 | tf_op jit(solution)/shard_map/ppermute | solution.py:561
  37.6 0.0 collective-permute-done.10.refs_5_
  37.6 0.0 collective-permute-done.12.refs_7_
  37.6 3.5 %shard_map.173 = bf16[32,32,128]{2,1,0:T(8,128)(2,1)} custom-call(bf16[16,1152]{1,0:T(8,128)(2,1)S(1)} %get-tuple-element.49.refs_0_, bf16[16,1152]{1,0:T(8,128)(2,1)S(1)} %collective-permute-done.6.refs_1_, bf16[16,1152]{1,0:T(8,128)(2,1)S(1)} %collective-permute-done.7.refs_2_, bf16[16,1152]{1,0:T(8,128)(2,1)S(1)} %collective-permute-done.8.refs_3_, ...), custom_call_target="tpu_custom_call" | custom-call | flops 1073741824 | bytes 4194304 | tf_op jit(solution)/shard_map/pallas_call | solution.py:57
  (1 shorter events, 0.0 us)
Async XLA Ops:
  2.2 9.5 %collective-permute-start.4 = (bf16[528,256]{1,0:T(8,128)(2,1)S(1)}, bf16[528,256]{1,0:T(8,128)(2,1)S(1)}, u32[]{:S(2)}, u32[]{:S(2)}) collective-permute-start(bf16[528,256]{1,0:T(8,128)(2,1)S(1)} %get-tuple-element.31.refs_0_), channel_id=1, source_target_pairs={{0,2},{2,0},{1,3},{3,1},{4,6},{6,4},{5,7},{7,5},{8,10},{10,8},{9,1... | collective-permute-start | bytes 811016 | tf_op jit(solution)/shard_map/ppermute | solution.py:482
  5.2 12.9 %collective-permute-start.3 = (bf16[528,256]{1,0:T(8,128)(2,1)S(1)}, bf16[528,256]{1,0:T(8,128)(2,1)S(1)}, u32[]{:S(2)}, u32[]{:S(2)}) collective-permute-start(bf16[528,256]{1,0:T(8,128)(2,1)S(1)} %get-tuple-element.31.refs_0_), channel_id=1, source_target_pairs={{0,1},{1,0},{2,3},{3,2},{4,5},{5,4},{6,7},{7,6},{8,9},{9,8},{10,11... | collective-permute-start | bytes 811016 | tf_op jit(solution)/shard_map/ppermute | solution.py:482
  11.7 7.1 %collective-permute-start.5 = (bf16[528,256]{1,0:T(8,128)(2,1)S(1)}, bf16[528,256]{1,0:T(8,128)(2,1)S(1)}, u32[]{:S(2)}, u32[]{:S(2)}) collective-permute-start(bf16[528,256]{1,0:T(8,128)(2,1)S(1)} %collective-permute-done.4.refs_2_), channel_id=1, source_target_pairs={{0,1},{1,0},{2,3},{3,2},{4,5},{5,4},{6,7},{7,6},{8,9},{9,8},{10,11... | collective-permute-start | bytes 811016 | tf_op jit(solution)/shard_map/ppermute | solution.py:482
  13.6 6.3 %collective-permute-start = (f32[8,1024]{1,0:T(8,128)S(1)}, f32[8,1024]{1,0:T(8,128)S(1)}, u32[]{:S(2)}, u32[]{:S(2)}) collective-permute-start(f32[8,1024]{1,0:T(8,128)S(1)} %get-tuple-element.30.refs_0_), channel_id=1, source_target_pairs={{0,4},{4,0},{8,12},{12,8},{1,5},{5,1},{9,13},{13,9},{2,6},{6,2},{1... | collective-permute-start | bytes 98312 | tf_op jit(solution)/shard_map/ppermute | solution.py:515
  15.5 5.3 %collective-permute-start.1 = (f32[8,1024]{1,0:T(8,128)S(1)}, f32[8,1024]{1,0:T(8,128)S(1)}, u32[]{:S(2)}, u32[]{:S(2)}) collective-permute-start(f32[8,1024]{1,0:T(8,128)S(1)} %get-tuple-element.30.refs_0_), channel_id=1, source_target_pairs={{0,8},{4,12},{8,0},{12,4},{1,9},{5,13},{9,1},{13,5},{2,10},{6,14},... | collective-permute-start | bytes 98312 | tf_op jit(solution)/shard_map/ppermute | solution.py:515
  18.1 5.7 %collective-permute-start.2 = (f32[8,1024]{1,0:T(8,128)S(1)}, f32[8,1024]{1,0:T(8,128)S(1)}, u32[]{:S(2)}, u32[]{:S(2)}) collective-permute-start(f32[8,1024]{1,0:T(8,128)S(1)} %get-tuple-element.30.refs_0_), channel_id=1, source_target_pairs={{0,12},{4,8},{8,4},{12,0},{1,13},{5,9},{9,5},{13,1},{2,14},{6,10},... | collective-permute-start | bytes 98312 | tf_op jit(solution)/shard_map/ppermute | solution.py:515
  25.8 7.9 %collective-permute-start.9 = (bf16[16,1152]{1,0:T(8,128)(2,1)S(1)}, bf16[16,1152]{1,0:T(8,128)(2,1)S(1)}, u32[]{:S(2)}, u32[]{:S(2)}) collective-permute-start(bf16[16,1152]{1,0:T(8,128)(2,1)S(1)} %get-tuple-element.50), channel_id=1, source_target_pairs={{0,0},{1,4},{2,8},{3,12},{4,1},{5,5},{6,9},{7,13},{8,2},{9,6},{10,... | collective-permute-start | bytes 110600 | tf_op jit(solution)/shard_map/ppermute | solution.py:570
  26.5 8.8 %collective-permute-start.11 = (bf16[16,1152]{1,0:T(8,128)(2,1)S(1)}, bf16[16,1152]{1,0:T(8,128)(2,1)S(1)}, u32[]{:S(2)}, u32[]{:S(2)}) collective-permute-start(bf16[16,1152]{1,0:T(8,128)(2,1)S(1)} %get-tuple-element.50), channel_id=1, source_target_pairs={{0,2},{1,6},{2,10},{3,14},{4,3},{5,7},{6,11},{7,15},{8,0},{9,4},{1... | collective-permute-start | bytes 110600 | tf_op jit(solution)/shard_map/ppermute | solution.py:570
  29.3 6.1 %collective-permute-start.6 = (bf16[16,1152]{1,0:T(8,128)(2,1)S(1)}, bf16[16,1152]{1,0:T(8,128)(2,1)S(1)}, u32[]{:S(2)}, u32[]{:S(2)}) collective-permute-start(bf16[16,1152]{1,0:T(8,128)(2,1)S(1)} %get-tuple-element.49.refs_0_), channel_id=1, source_target_pairs={{0,4},{4,0},{8,12},{12,8},{1,5},{5,1},{9,13},{13,9},{2,6},{6,2},{1... | collective-permute-start | bytes 110600 | tf_op jit(solution)/shard_map/ppermute | solution.py:561
  30.9 5.2 %collective-permute-start.7 = (bf16[16,1152]{1,0:T(8,128)(2,1)S(1)}, bf16[16,1152]{1,0:T(8,128)(2,1)S(1)}, u32[]{:S(2)}, u32[]{:S(2)}) collective-permute-start(bf16[16,1152]{1,0:T(8,128)(2,1)S(1)} %get-tuple-element.49.refs_0_), channel_id=1, source_target_pairs={{0,8},{4,12},{8,0},{12,4},{1,9},{5,13},{9,1},{13,5},{2,10},{6,14},... | collective-permute-start | bytes 110600 | tf_op jit(solution)/shard_map/ppermute | solution.py:561
  31.8 5.8 %collective-permute-start.8 = (bf16[16,1152]{1,0:T(8,128)(2,1)S(1)}, bf16[16,1152]{1,0:T(8,128)(2,1)S(1)}, u32[]{:S(2)}, u32[]{:S(2)}) collective-permute-start(bf16[16,1152]{1,0:T(8,128)(2,1)S(1)} %get-tuple-element.49.refs_0_), channel_id=1, source_target_pairs={{0,12},{4,8},{8,4},{12,0},{1,13},{5,9},{9,5},{13,1},{2,14},{6,10},... | collective-permute-start | bytes 110600 | tf_op jit(solution)/shard_map/ppermute | solution.py:561
  33.7 3.9 %collective-permute-start.10 = (bf16[16,1152]{1,0:T(8,128)(2,1)S(1)}, bf16[16,1152]{1,0:T(8,128)(2,1)S(1)}, u32[]{:S(2)}, u32[]{:S(2)}) collective-permute-start(bf16[16,1152]{1,0:T(8,128)(2,1)S(1)} %collective-permute-done.9.refs_4_), channel_id=1, source_target_pairs={{0,1},{1,0},{2,3},{3,2},{4,5},{5,4},{6,7},{7,6},{8,9},{9,8},{10,11... | collective-permute-start | bytes 110600 | tf_op jit(solution)/shard_map/ppermute | solution.py:482
  35.3 2.3 %collective-permute-start.12 = (bf16[16,1152]{1,0:T(8,128)(2,1)S(1)}, bf16[16,1152]{1,0:T(8,128)(2,1)S(1)}, u32[]{:S(2)}, u32[]{:S(2)}) collective-permute-start(bf16[16,1152]{1,0:T(8,128)(2,1)S(1)} %collective-permute-done.11.refs_6_), channel_id=1, source_target_pairs={{0,1},{1,0},{2,3},{3,2},{4,5},{5,4},{6,7},{7,6},{8,9},{9,8},{10,11... | collective-permute-start | bytes 110600 | tf_op jit(solution)/shard_map/ppermute | solution.py:482

commit v2 on v1

--- a/solution.py
+++ b/solution.py
@@ -41,7 +41,7 @@
     return (iota((rows, columns), 1) % rows == iota((rows, columns), 0)).astype(BF16)
 
 
-def call(body, outs, scratch=(), flops=0, data=0, far=0, aliases={}):
+def call(body, outs, scratch=(), flops=0, data=0, far=0, aliases={}, sent=()):
     near = pl.BlockSpec(memory_space=pltpu.VMEM)
     held = sum(
         math.prod(ref.shape) * jnp.dtype(ref.dtype).itemsize
@@ -58,7 +58,10 @@
             body,
             out_shape=outs,
             in_specs=[pl.BlockSpec(memory_space=pltpu.HBM)] * far + [near] * (len(operands) - far),
-            out_specs=jax.tree.map(lambda _: near, outs),
+            out_specs=[
+                pl.BlockSpec(memory_space=pltpu.HBM) if n in sent else near
+                for n in range(len(outs))
+            ],
             scratch_shapes=scratch,
             cost_estimate=pl.CostEstimate(flops=flops, bytes_accessed=data, transcendentals=0),
             compiler_params=pltpu.CompilerParams(vmem_limit_bytes=held * 5 // 4 + (6 << 20)),
@@ -129,22 +132,38 @@
         copy.wait()
 
 
+def thirds(values):
+    high = values.astype(BF16)
+    rest = values - high.astype(F32)
+    middle = rest.astype(BF16)
+    return [high, middle, (rest - middle.astype(F32)).astype(BF16)]
+
+
 def prepare_kernel(weights, *refs):
     far, (pair_ref, matrix_ref), refs = refs[:weights], refs[weights : weights + 2], refs[weights + 2 :]
     near, (out_ref, sems) = refs[:weights], refs[weights:]
     copies = fetch(far, near, sems)
     rows, columns, width = pair_ref.shape
-    matrix = matrix_ref[...]
+    matrix = thirds(matrix_ref[...])
+    stacked = jnp.concatenate([jnp.concatenate(matrix, axis=0)] * len(matrix), axis=1)
+    heads = matrix_ref.shape[0]
     step = LANES // columns
     for start in range(0, rows, step):
         part = pair_ref[start : start + step].reshape(step * columns, width).astype(F32)
-        bias = dot(matrix, standardize(part), (1, 1), lax.Precision.HIGHEST)
+        products = dot(stacked, jnp.concatenate(thirds(standardize(part)), axis=1), (1, 1))
+        bias = products[2 * heads :] + products[heads : 2 * heads] + products[:heads]
         out_ref[:, start * columns : (start + step) * columns] = bias
     for copy in copies:
         copy.wait()
 
 
-def block_kernel(mix_ref, block_ref, wide):
+def block_kernel(
+    mix_far, w1_far, w2_far, profile_ref, block_ref, w1_ref, w2_ref, profile_far, mix_ref, wide, sems
+):
+    copies = fetch(
+        (mix_far, w1_far, w2_far, profile_ref), (mix_ref, w1_ref, w2_ref, profile_far), sems
+    )
+    copies[0].wait()
     turns = block_ref.shape[0]
     width = other = math.isqrt(mix_ref.shape[0])
     pitch = wide.shape[0] // width
@@ -156,6 +175,8 @@
         for turn in range(turns):
             spot = (high * turns + (low + turn) % turns) * width
             block_ref[turn, spot : spot + width, :] = piece
+    for copy in copies[1:]:
+        copy.wait()
 
 
 def block_rows(shift, residues):
@@ -351,7 +372,7 @@
 def pair_kernel(left_from, right_from, *refs):
     lefts = refs[: len(left_from)]
     rights = refs[len(left_from) : len(left_from) + len(right_from)]
-    (pair_ref, block_ref, w1_ref, w2_ref, out_ref, left, right, flipped, spread, stacked, middle, normed) = refs[
+    (pair_ref, block_ref, w1_ref, w2_ref, out_ref, left, right, flipped, rolled, spread, stacked, middle, normed) = refs[
         len(left_from) + len(right_from) :
     ]
     sequences = lefts[0].shape[0]
@@ -378,15 +399,21 @@
         [right[:, low * span : (low + 1) * span] for low in range(fit)]
     ).T
     group = iota((deep, LANES), 1) // width
+    lane_groups = [group == q for q in range(fit)]
     for tile in range(tiles):
         lanes = slice(tile * LANES, (tile + 1) * LANES)
         chunk = left[:, lanes].astype(F32)
+        for low in range(1, fit):
+            rolled[low - 1, :, lanes] = pltpu.roll(chunk, low * width, 1).astype(BF16)
+
+    def build(turn):
         for low in range(fit):
-            rolled = pltpu.roll(chunk, low * width, 1) if low else chunk
-            for turn in range(fit):
+            for tile in range(tiles):
+                lanes = slice(tile * LANES, (tile + 1) * LANES)
+                chunk = rolled[low - 1, :, lanes] if low else left[:, lanes]
                 spread[turn, low * deep : (low + 1) * deep, lanes] = jnp.where(
-                    group == (low + turn) % fit, rolled, 0.0
-                ).astype(BF16)
+                    lane_groups[(low + turn) % fit], chunk, jnp.zeros_like(chunk)
+                )
 
     def outer(turn):
         value = dot(flipped[...], spread[turn]).astype(BF16)
@@ -412,7 +439,7 @@
         for tile in range(tiles):
             out_ref[tile * fit + turn] = done[tile * columns : (tile + 1) * columns, :]
 
-    stages = (outer, mix, norm, transition)
+    stages = (build, outer, mix, norm, transition)
     for step in range(fit + len(stages) - 1):
         for late, stage in reversed(list(enumerate(stages))):
             if 0 <= step - late < fit:
@@ -497,11 +524,8 @@
         resulting_weights,
         first_factor_weights.T,
         second_factor_weights.T,
-        widening_weight,
-        narrowing_weight,
-        outer_mixing_weight,
-    )
-    wq, wk, wv, wg, wr, wf, ws, w1, w2, mix, bias_local = call(
+    )
+    wq, wk, wv, wg, wr, wf, ws, bias_local = call(
         functools.partial(prepare_kernel, len(weights)),
         tuple(shape(w.shape, w.dtype) for w in weights)
         + (shape((heads, pair_rows * pair_columns), F32),),
@@ -572,21 +596,31 @@
             right_from.append((r, t, size_y, size_z))
             rights.append(got if t == 0 else shift(got, "gz", size_z, t))
 
-    block = call(
+    mixing = (outer_mixing_weight, widening_weight, narrowing_weight)
+    block, w1, w2, refreshed = call(
         block_kernel,
-        shape((fit, width * width, pair_width), BF16),
-        [pltpu.VMEM((width * (width + SKEW), pair_width), F32)],
+        (shape((fit, width * width, pair_width), BF16),)
+        + tuple(shape(w.shape, w.dtype) for w in mixing[1:])
+        + (shape(three, BF16),),
+        [
+            pltpu.VMEM(outer_mixing_weight.shape, BF16),
+            pltpu.VMEM((width * (width + SKEW), pair_width), F32),
+            pltpu.SemaphoreType.DMA((len(mixing) + 1,)),
+        ],
         data=width * width * fit * pair_width * 2,
-    )(mix)
+        far=len(mixing),
+        sent=(3,),
+    )(*mixing, refreshed)
 
     depth = sequences * size_x
-    pair_output = call(
+    (pair_output,) = call(
         functools.partial(pair_kernel, tuple(range(size_x)), tuple(right_from)),
-        shape(pair_features.shape, BF16),
+        (shape(pair_features.shape, BF16),),
         [
             pltpu.VMEM((depth, wide + LANES), BF16),
             pltpu.VMEM((depth, wide + LANES), BF16),
             pltpu.VMEM((width // fit * pair_columns, fit * depth), BF16),
+            pltpu.VMEM((fit - 1, depth, wide), BF16),
             pltpu.VMEM((fit, fit * depth, wide), BF16),
             pltpu.VMEM((fit, pair_rows // fit * pair_columns, width * width), BF16),
             pltpu.VMEM((fit, pair_rows // fit * pair_columns, pair_width), F32),

time: 41.2 us -> 40.7 us (0.988)
  waiting for transfers between devices: 14.1 us -> 13 us
  Pallas kernels: 10.8 us -> 11.3 us
    ppermute x3, waiting for transfers between devices: 2.14 us -> 1.05 us  [local(): lax.ppermute(left_own, 'gx', [(n, n ^ m) for n in range(size_x)])]
    pallas_call x7, Pallas kernels: 10.8 us -> 11.3 us  [run(): pl.pallas_call(body, out_shape=outs, in_specs=[pl.BlockSpec(memory_space=...]
  transfers between devices with their start and end apart: 13 -> 13, of which waited for: 6 -> 5; matrix products, arithmetic and copies ran while one was open for 0% -> 0% of each run, Pallas kernels for 9% -> 11%
where the time goes in v2:
time: 40.7 us; the launch traced here: 40.4 us
  starting transfers between devices  15.4 us (38%)
  waiting for transfers between devices  13 us (32%)
  Pallas kernels  11.3 us (28%)
  between operations  0.72 us (2%)
    pallas_call x7, Pallas kernels, run(): pl.pallas_call(body, out_shape=outs, in_specs=[pl.BlockSpec(memory_space=...  11.3 us
    ppermute x5, waiting for transfers between devices, shift(): lax.ppermute(value, axis, [(n, (n + step) % count) for n in range(count)])  6.49 us
    ppermute x3, starting transfers between devices, local(): lax.ppermute(bias_local, 'gx', [(n, n ^ m) for n in range(size_x)])  4.48 us
    ppermute x3, starting transfers between devices, local(): lax.ppermute(left_own, 'gx', [(n, n ^ m) for n in range(size_x)])  4.39 us
    ppermute x3, waiting for transfers between devices, local(): lax.ppermute(bias_local, 'gx', [(n, n ^ m) for n in range(size_x)])  3.89 us
    ppermute x2, starting transfers between devices, local(): got = lax.ppermute(right_own, ('gx', 'gy', 'gz'), pairs)  3.47 us
    ppermute x5, starting transfers between devices, shift(): lax.ppermute(value, axis, [(n, (n + step) % count) for n in range(count)])  3.04 us
    ppermute x2, waiting for transfers between devices, local(): got = lax.ppermute(right_own, ('gx', 'gy', 'gz'), pairs)  1.6 us
  transfers between devices with their start and end apart: 13, of which 5 were waited for; matrix products, arithmetic and copies ran while one was open for 0% of the time, Pallas kernels for 11%

profile of v2, /device:TPU:0, one launch (start us, length us, event | category | flops | bytes accessed | tf_op | source)
XLA Modules:
  0.0 40.4 jit_solution(14386234715403412001)
XLA Ops:
  0.6 1.5 %shard_map.167 = (bf16[528,256]{1,0:T(8,128)(2,1)S(1)}, f32[512,256]{1,0:T(8,128)S(1)}, s32[16,32]{1,0:T(8,128)S(1)}, bf16[32,32,128]{2,1,0:T(8,128)(2,1)S(1)}, f32[8,128]{1,0:T(8,128)S(1)}) custom-call(s32[16,32]{1,0:T(8,128)} %ids_far.1, s32[16,32]{1,0:T(8,128)} %mask_far.1, bf16[16,32,256]{2,1,0:T(8,128)(2,1)} %profile_far.1, bf16[23,256]{1,0:T(8,128)(2,1)} %table_far.1, ...), custom_call_target="tpu_custom_call" | custom-call | flops 33554432 | bytes 1048576 | tf_op jit(solution)/shard_map/pallas_call | solution.py:57
  2.2 3.0 %collective-permute-start.4 = (bf16[528,256]{1,0:T(8,128)(2,1)S(1)}, bf16[528,256]{1,0:T(8,128)(2,1)S(1)}, u32[]{:S(2)}, u32[]{:S(2)}) collective-permute-start(bf16[528,256]{1,0:T(8,128)(2,1)S(1)} %get-tuple-element.32.refs_0_), channel_id=1, source_target_pairs={{0,2},{2,0},{1,3},{3,1},{4,6},{6,4},{5,7},{7,5},{8,10},{10,8},{9,1... | collective-permute-start | bytes 811016 | tf_op jit(solution)/shard_map/ppermute | solution.py:509
  5.2 0.0 collective-permute-start.3
  5.2 6.5 %collective-permute-done.4.refs_2_ = bf16[528,256]{1,0:T(8,128)(2,1)S(1)} collective-permute-done((bf16[528,256]{1,0:T(8,128)(2,1)S(1)}, bf16[528,256]{1,0:T(8,128)(2,1)S(1)}, u32[]{:S(2)}, u32[]{:S(2)}) %collective-permute-start.4) | collective-permute-done | bytes 270368 | tf_op jit(solution)/shard_map/ppermute | solution.py:509
  11.7 0.0 collective-permute-start.5
  11.7 1.4 %shard_map.168 = (bf16[256,256]{1,0:T(8,128)(2,1)S(1)}, bf16[256,256]{1,0:T(8,128)(2,1)S(1)}, bf16[256,256]{1,0:T(8,128)(2,1)S(1)}, bf16[256,256]{1,0:T(8,128)(2...) custom-call(bf16[256,256]{1,0:T(8,128)(2,1)} %refs_0_.1, ...), custom_call_target="tpu_custom_call" | custom-call | flops 201326592 | bytes 262144 | tf_op jit(solution)/shard_map/pallas_call | solution.py:57
  13.0 1.9 %collective-permute-start = (f32[8,1024]{1,0:T(8,128)S(1)}, f32[8,1024]{1,0:T(8,128)S(1)}, u32[]{:S(2)}, u32[]{:S(2)}) collective-permute-start(f32[8,1024]{1,0:T(8,128)S(1)} %get-tuple-element.31.refs_0_), channel_id=1, source_target_pairs={{0,4},{4,0},{8,12},{12,8},{1,5},{5,1},{9,13},{13,9},{2,6},{6,2},{1... | collective-permute-start | bytes 98312 | tf_op jit(solution)/shard_map/ppermute | solution.py:539
  14.9 2.6 %collective-permute-start.1 = (f32[8,1024]{1,0:T(8,128)S(1)}, f32[8,1024]{1,0:T(8,128)S(1)}, u32[]{:S(2)}, u32[]{:S(2)}) collective-permute-start(f32[8,1024]{1,0:T(8,128)S(1)} %get-tuple-element.31.refs_0_), channel_id=1, source_target_pairs={{0,8},{4,12},{8,0},{12,4},{1,9},{5,13},{9,1},{13,5},{2,10},{6,14},... | collective-permute-start | bytes 98312 | tf_op jit(solution)/shard_map/ppermute | solution.py:539
  17.5 0.0 collective-permute-start.2
  17.5 0.0 collective-permute-done.3.refs_1_
  17.5 0.7 %shard_map.169 = (bf16[16,32,256]{2,1,0:T(8,128)(2,1)S(1)}, bf16[16,128,256]{2,1,0:T(8,128)(2,1)S(1)}, bf16[16,128,256]{2,1,0:T(8,128)(2,1)S(1)}, f32[16,32,256]{2,1,0:T(8,128)S(1)}) custom-call(bf16[528,256]{1,0:T(8,128)(2,1)S(1)} %get-tuple-element.32.refs_0_, bf16[528,256]{1,0:T(8,128)(2,1)S(1)} %collective-permute-done.3.refs_1_, ...), custom_call_target="tpu_custom_call" | custom-call | flops 536870912 | bytes 3145728 | tf_op jit(solution)/shard_map/pallas_call | solution.py:57
  18.3 0.0 collective-permute-done.5.refs_3_
  18.3 1.1 %shard_map.170 = (bf16[16,128,256]{2,1,0:T(8,128)(2,1)S(1)}, bf16[16,128,256]{2,1,0:T(8,128)(2,1)S(1)}, f32[16,256,128]{2,1,0:T(8,128)S(1)}, f32[16,128]{1,0:T(8,128)S(1)}) custom-call(bf16[528,256]{1,0:T(8,128)(2,1)S(1)} %get-tuple-element.32.refs_0_, ...), custom_call_target="tpu_custom_call", output_to_operand_aliasing={{0}: (5, {}), {1}: (6, {})} | custom-call | flops 134217728 | bytes 3145728 | tf_op jit(solution)/shard_map/pallas_call | solution.py:57
  19.3 0.9 %collective-permute-done.1.refs_2_ = f32[8,1024]{1,0:T(8,128)S(1)} collective-permute-done((f32[8,1024]{1,0:T(8,128)S(1)}, f32[8,1024]{1,0:T(8,128)S(1)}, u32[]{:S(2)}, u32[]{:S(2)}) %collective-permute-start.1) | collective-permute-done | bytes 32800 | tf_op jit(solution)/shard_map/ppermute | solution.py:539
  20.3 3.0 %collective-permute-done.2.refs_3_ = f32[8,1024]{1,0:T(8,128)S(1)} collective-permute-done((f32[8,1024]{1,0:T(8,128)S(1)}, f32[8,1024]{1,0:T(8,128)S(1)}, u32[]{:S(2)}, u32[]{:S(2)}) %collective-permute-start.2) | collective-permute-done | bytes 32800 | tf_op jit(solution)/shard_map/ppermute | solution.py:539
  23.2 2.0 %shard_map.171 = (bf16[16,32,256]{2,1,0:T(8,128)(2,1)S(1)}, bf16[16,1152]{1,0:T(8,128)(2,1)S(1)}, bf16[16,1152]{1,0:T(8,128)(2,1)S(1)}) custom-call(f32[8,1024]{1,0:T(8,128)S(1)} %get-tuple-element.31.refs_0_, f32[8,1024]{1,0:T(8,128)S(1)} %collective-permute-done.refs_1_, f32[8,1024]{1,0:T(8,128)S(1)} %collective-permute-done.1.refs_2_, ...), custom_call_target="tpu_custom_call" | custom-call | flops 268435456 | bytes 2097152 | tf_op jit(solution)/shard_map/pallas_call | solution.py:57
  25.3 0.7 %collective-permute-start.9 = (bf16[16,1152]{1,0:T(8,128)(2,1)S(1)}, bf16[16,1152]{1,0:T(8,128)(2,1)S(1)}, u32[]{:S(2)}, u32[]{:S(2)}) collective-permute-start(bf16[16,1152]{1,0:T(8,128)(2,1)S(1)} %get-tuple-element.52), channel_id=1, source_target_pairs={{0,0},{1,4},{2,8},{3,12},{4,1},{5,5},{6,9},{7,13},{8,2},{9,6},{10,... | collective-permute-start | bytes 110600 | tf_op jit(solution)/shard_map/ppermute | solution.py:594
  25.9 2.8 %collective-permute-start.11 = (bf16[16,1152]{1,0:T(8,128)(2,1)S(1)}, bf16[16,1152]{1,0:T(8,128)(2,1)S(1)}, u32[]{:S(2)}, u32[]{:S(2)}) collective-permute-start(bf16[16,1152]{1,0:T(8,128)(2,1)S(1)} %get-tuple-element.52), channel_id=1, source_target_pairs={{0,2},{1,6},{2,10},{3,14},{4,3},{5,7},{6,11},{7,15},{8,0},{9,4},{1... | collective-permute-start | bytes 110600 | tf_op jit(solution)/shard_map/ppermute | solution.py:594
  28.7 1.6 %collective-permute-start.6 = (bf16[16,1152]{1,0:T(8,128)(2,1)S(1)}, bf16[16,1152]{1,0:T(8,128)(2,1)S(1)}, u32[]{:S(2)}, u32[]{:S(2)}) collective-permute-start(bf16[16,1152]{1,0:T(8,128)(2,1)S(1)} %get-tuple-element.51.refs_0_), channel_id=1, source_target_pairs={{0,4},{4,0},{8,12},{12,8},{1,5},{5,1},{9,13},{13,9},{2,6},{6,2},{1... | collective-permute-start | bytes 110600 | tf_op jit(solution)/shard_map/ppermute | solution.py:585
  30.3 1.0 %collective-permute-start.7 = (bf16[16,1152]{1,0:T(8,128)(2,1)S(1)}, bf16[16,1152]{1,0:T(8,128)(2,1)S(1)}, u32[]{:S(2)}, u32[]{:S(2)}) collective-permute-start(bf16[16,1152]{1,0:T(8,128)(2,1)S(1)} %get-tuple-element.51.refs_0_), channel_id=1, source_target_pairs={{0,8},{4,12},{8,0},{12,4},{1,9},{5,13},{9,1},{13,5},{2,10},{6,14},... | collective-permute-start | bytes 110600 | tf_op jit(solution)/shard_map/ppermute | solution.py:585
  31.2 1.9 %collective-permute-start.8 = (bf16[16,1152]{1,0:T(8,128)(2,1)S(1)}, bf16[16,1152]{1,0:T(8,128)(2,1)S(1)}, u32[]{:S(2)}, u32[]{:S(2)}) collective-permute-start(bf16[16,1152]{1,0:T(8,128)(2,1)S(1)} %get-tuple-element.51.refs_0_), channel_id=1, source_target_pairs={{0,12},{4,8},{8,4},{12,0},{1,13},{5,9},{9,5},{13,1},{2,14},{6,10},... | collective-permute-start | bytes 110600 | tf_op jit(solution)/shard_map/ppermute | solution.py:585
  33.1 0.0 collective-permute-done.9.refs_4_
  33.1 0.0 collective-permute-start.10
  33.1 1.6 %collective-permute-done.11.refs_6_ = bf16[16,1152]{1,0:T(8,128)(2,1)S(1)} collective-permute-done((bf16[16,1152]{1,0:T(8,128)(2,1)S(1)}, bf16[16,1152]{1,0:T(8,128)(2,1)S(1)}, u32[]{:S(2)}, u32[]{:S(2)}) %collective-permute-start.11) | collective-permute-done | bytes 36896 | tf_op jit(solution)/shard_map/ppermute | solution.py:594
  34.7 0.0 collective-permute-start.12
  34.7 1.2 %shard_map.172 = (bf16[4,1024,128]{2,1,0:T(8,128)(2,1)S(1)}, bf16[128,512]{1,0:T(8,128)(2,1)S(1)}, bf16[512,128]{1,0:T(8,128)(2,1)S(1)}, bf16[16,32,256]{2,1,0:T(8,128)(2,1)}) custom-call(bf16[1024,128]{1,0:T(8,128)(2,1)} %mix_far.1, bf16[128,512]{1,0:T(8,128)(2,1)} %w1_far.1, bf16[512,128]{1,0:T(8,128)(2,1)} %w2_far.1, ...), custom_call_target="tpu_custom_call" | custom-call | bytes 1048576 | tf_op jit(solution)/shard_map/pallas_call | solution.py:57
  35.9 0.0 collective-permute-done.6.refs_1_
  35.9 0.0 collective-permute-done.7.refs_2_
  35.9 1.0 %collective-permute-done.8.refs_3_ = bf16[16,1152]{1,0:T(8,128)(2,1)S(1)} collective-permute-done((bf16[16,1152]{1,0:T(8,128)(2,1)S(1)}, bf16[16,1152]{1,0:T(8,128)(2,1)S(1)}, u32[]{:S(2)}, u32[]{:S(2)}) %collective-permute-start.8) | collective-permute-done | bytes 36896 | tf_op jit(solution)/shard_map/ppermute | solution.py:585
  37.0 0.0 collective-permute-done.10.refs_5_
  37.0 0.0 collective-permute-done.12.refs_7_
  37.0 3.4 %shard_map.173 = bf16[32,32,128]{2,1,0:T(8,128)(2,1)} custom-call(bf16[16,1152]{1,0:T(8,128)(2,1)S(1)} %get-tuple-element.51.refs_0_, bf16[16,1152]{1,0:T(8,128)(2,1)S(1)} %collective-permute-done.6.refs_1_, bf16[16,1152]{1,0:T(8,128)(2,1)S(1)} %collective-permute-done.7.refs_2_, bf16[16,1152]{1,0:T(8,128)(2,1)S(1)} %collective-permute-done.8.refs_3_, ...), custom_call_target="tpu_custom_call" | custom-call | flops 1073741824 | bytes 4194304 | tf_op jit(solution)/shard_map/pallas_call | solution.py:57
  (1 shorter events, 0.0 us)
Async XLA Ops:
  2.2 9.5 %collective-permute-start.4 = (bf16[528,256]{1,0:T(8,128)(2,1)S(1)}, bf16[528,256]{1,0:T(8,128)(2,1)S(1)}, u32[]{:S(2)}, u32[]{:S(2)}) collective-permute-start(bf16[528,256]{1,0:T(8,128)(2,1)S(1)} %get-tuple-element.32.refs_0_), channel_id=1, source_target_pairs={{0,2},{2,0},{1,3},{3,1},{4,6},{6,4},{5,7},{7,5},{8,10},{10,8},{9,1... | collective-permute-start | bytes 811016 | tf_op jit(solution)/shard_map/ppermute | solution.py:509
  5.2 12.3 %collective-permute-start.3 = (bf16[528,256]{1,0:T(8,128)(2,1)S(1)}, bf16[528,256]{1,0:T(8,128)(2,1)S(1)}, u32[]{:S(2)}, u32[]{:S(2)}) collective-permute-start(bf16[528,256]{1,0:T(8,128)(2,1)S(1)} %get-tuple-element.32.refs_0_), channel_id=1, source_target_pairs={{0,1},{1,0},{2,3},{3,2},{4,5},{5,4},{6,7},{7,6},{8,9},{9,8},{10,11... | collective-permute-start | bytes 811016 | tf_op jit(solution)/shard_map/ppermute | solution.py:509
  11.7 6.6 %collective-permute-start.5 = (bf16[528,256]{1,0:T(8,128)(2,1)S(1)}, bf16[528,256]{1,0:T(8,128)(2,1)S(1)}, u32[]{:S(2)}, u32[]{:S(2)}) collective-permute-start(bf16[528,256]{1,0:T(8,128)(2,1)S(1)} %collective-permute-done.4.refs_2_), channel_id=1, source_target_pairs={{0,1},{1,0},{2,3},{3,2},{4,5},{5,4},{6,7},{7,6},{8,9},{9,8},{10,11... | collective-permute-start | bytes 811016 | tf_op jit(solution)/shard_map/ppermute | solution.py:509
  13.0 6.3 %collective-permute-start = (f32[8,1024]{1,0:T(8,128)S(1)}, f32[8,1024]{1,0:T(8,128)S(1)}, u32[]{:S(2)}, u32[]{:S(2)}) collective-permute-start(f32[8,1024]{1,0:T(8,128)S(1)} %get-tuple-element.31.refs_0_), channel_id=1, source_target_pairs={{0,4},{4,0},{8,12},{12,8},{1,5},{5,1},{9,13},{13,9},{2,6},{6,2},{1... | collective-permute-start | bytes 98312 | tf_op jit(solution)/shard_map/ppermute | solution.py:539
  14.9 5.3 %collective-permute-start.1 = (f32[8,1024]{1,0:T(8,128)S(1)}, f32[8,1024]{1,0:T(8,128)S(1)}, u32[]{:S(2)}, u32[]{:S(2)}) collective-permute-start(f32[8,1024]{1,0:T(8,128)S(1)} %get-tuple-element.31.refs_0_), channel_id=1, source_target_pairs={{0,8},{4,12},{8,0},{12,4},{1,9},{5,13},{9,1},{13,5},{2,10},{6,14},... | collective-permute-start | bytes 98312 | tf_op jit(solution)/shard_map/ppermute | solution.py:539
  17.5 5.7 %collective-permute-start.2 = (f32[8,1024]{1,0:T(8,128)S(1)}, f32[8,1024]{1,0:T(8,128)S(1)}, u32[]{:S(2)}, u32[]{:S(2)}) collective-permute-start(f32[8,1024]{1,0:T(8,128)S(1)} %get-tuple-element.31.refs_0_), channel_id=1, source_target_pairs={{0,12},{4,8},{8,4},{12,0},{1,13},{5,9},{9,5},{13,1},{2,14},{6,10},... | collective-permute-start | bytes 98312 | tf_op jit(solution)/shard_map/ppermute | solution.py:539
  25.3 7.9 %collective-permute-start.9 = (bf16[16,1152]{1,0:T(8,128)(2,1)S(1)}, bf16[16,1152]{1,0:T(8,128)(2,1)S(1)}, u32[]{:S(2)}, u32[]{:S(2)}) collective-permute-start(bf16[16,1152]{1,0:T(8,128)(2,1)S(1)} %get-tuple-element.52), channel_id=1, source_target_pairs={{0,0},{1,4},{2,8},{3,12},{4,1},{5,5},{6,9},{7,13},{8,2},{9,6},{10,... | collective-permute-start | bytes 110600 | tf_op jit(solution)/shard_map/ppermute | solution.py:594
  25.9 8.8 %collective-permute-start.11 = (bf16[16,1152]{1,0:T(8,128)(2,1)S(1)}, bf16[16,1152]{1,0:T(8,128)(2,1)S(1)}, u32[]{:S(2)}, u32[]{:S(2)}) collective-permute-start(bf16[16,1152]{1,0:T(8,128)(2,1)S(1)} %get-tuple-element.52), channel_id=1, source_target_pairs={{0,2},{1,6},{2,10},{3,14},{4,3},{5,7},{6,11},{7,15},{8,0},{9,4},{1... | collective-permute-start | bytes 110600 | tf_op jit(solution)/shard_map/ppermute | solution.py:594
  28.7 7.2 %collective-permute-start.6 = (bf16[16,1152]{1,0:T(8,128)(2,1)S(1)}, bf16[16,1152]{1,0:T(8,128)(2,1)S(1)}, u32[]{:S(2)}, u32[]{:S(2)}) collective-permute-start(bf16[16,1152]{1,0:T(8,128)(2,1)S(1)} %get-tuple-element.51.refs_0_), channel_id=1, source_target_pairs={{0,4},{4,0},{8,12},{12,8},{1,5},{5,1},{9,13},{13,9},{2,6},{6,2},{1... | collective-permute-start | bytes 110600 | tf_op jit(solution)/shard_map/ppermute | solution.py:585
  30.3 5.7 %collective-permute-start.7 = (bf16[16,1152]{1,0:T(8,128)(2,1)S(1)}, bf16[16,1152]{1,0:T(8,128)(2,1)S(1)}, u32[]{:S(2)}, u32[]{:S(2)}) collective-permute-start(bf16[16,1152]{1,0:T(8,128)(2,1)S(1)} %get-tuple-element.51.refs_0_), channel_id=1, source_target_pairs={{0,8},{4,12},{8,0},{12,4},{1,9},{5,13},{9,1},{13,5},{2,10},{6,14},... | collective-permute-start | bytes 110600 | tf_op jit(solution)/shard_map/ppermute | solution.py:585
  31.2 5.8 %collective-permute-start.8 = (bf16[16,1152]{1,0:T(8,128)(2,1)S(1)}, bf16[16,1152]{1,0:T(8,128)(2,1)S(1)}, u32[]{:S(2)}, u32[]{:S(2)}) collective-permute-start(bf16[16,1152]{1,0:T(8,128)(2,1)S(1)} %get-tuple-element.51.refs_0_), channel_id=1, source_target_pairs={{0,12},{4,8},{8,4},{12,0},{1,13},{5,9},{9,5},{13,1},{2,14},{6,10},... | collective-permute-start | bytes 110600 | tf_op jit(solution)/shard_map/ppermute | solution.py:585
  33.1 3.9 %collective-permute-start.10 = (bf16[16,1152]{1,0:T(8,128)(2,1)S(1)}, bf16[16,1152]{1,0:T(8,128)(2,1)S(1)}, u32[]{:S(2)}, u32[]{:S(2)}) collective-permute-start(bf16[16,1152]{1,0:T(8,128)(2,1)S(1)} %collective-permute-done.9.refs_4_), channel_id=1, source_target_pairs={{0,1},{1,0},{2,3},{3,2},{4,5},{5,4},{6,7},{7,6},{8,9},{9,8},{10,11... | collective-permute-start | bytes 110600 | tf_op jit(solution)/shard_map/ppermute | solution.py:509
  34.7 2.3 %collective-permute-start.12 = (bf16[16,1152]{1,0:T(8,128)(2,1)S(1)}, bf16[16,1152]{1,0:T(8,128)(2,1)S(1)}, u32[]{:S(2)}, u32[]{:S(2)}) collective-permute-start(bf16[16,1152]{1,0:T(8,128)(2,1)S(1)} %collective-permute-done.11.refs_6_), channel_id=1, source_target_pairs={{0,1},{1,0},{2,3},{3,2},{4,5},{5,4},{6,7},{7,6},{8,9},{9,8},{10,11... | collective-permute-start | bytes 110600 | tf_op jit(solution)/shard_map/ppermute | solution.py:509

commit v3 on v2

--- a/solution.py
+++ b/solution.py
@@ -10,7 +10,7 @@
 
 
 LANES = 128
-LAG = 4
+LAG = 8
 SKEW = 4
 SKEW_SMALL = 1
 F32 = jnp.float32
@@ -140,13 +140,19 @@
 
 
 def prepare_kernel(weights, *refs):
-    far, (pair_ref, matrix_ref), refs = refs[:weights], refs[weights : weights + 2], refs[weights + 2 :]
+    far, refs = refs[:weights], refs[weights:]
+    (pair_ref, matrix_ref, mask_ref), refs = refs[:3], refs[3:]
     near, (out_ref, sems) = refs[:weights], refs[weights:]
     copies = fetch(far, near, sems)
     rows, columns, width = pair_ref.shape
     matrix = thirds(matrix_ref[...])
     stacked = jnp.concatenate([jnp.concatenate(matrix, axis=0)] * len(matrix), axis=1)
     heads = matrix_ref.shape[0]
+    sequences, residues = mask_ref.shape
+    out_ref[:, rows * columns :] = jnp.zeros((heads, LANES), F32)
+    for n in range(sequences // heads):
+        lane = rows * columns + n * residues
+        out_ref[:, lane : lane + residues] = mask_ref[n * heads : (n + 1) * heads, :].astype(F32)
     step = LANES // columns
     for start in range(0, rows, step):
         part = pair_ref[start : start + step].reshape(step * columns, width).astype(F32)
@@ -271,7 +277,7 @@
     pitch = spread.shape[1] // residues
     z_own = lax.axis_index("gx")
     for other, ref in enumerate(biases):
-        bias_ref[z_own ^ other] = ref[...]
+        bias_ref[z_own ^ other] = ref[:, : bias_ref.shape[2]]
     lane = iota((heads, LANES), 1) // residues
     for i in range(residues):
         tile, inner = divmod(i, fit)
@@ -365,14 +371,14 @@
                 other = source[pl.ds(order[tile * count + p], sequences, stride=pitch), :]
                 value = other if p == 0 else jnp.where(group == p, other, value)
             target[:, lanes] = (value * present).astype(BF16)
-    left_ref[:, wide:] = right_mask.astype(BF16)
     right_ref[:, wide:] = right_mask.astype(BF16)
 
 
 def pair_kernel(left_from, right_from, *refs):
+    biases, refs = refs[: len(left_from)], refs[len(left_from) :]
     lefts = refs[: len(left_from)]
     rights = refs[len(left_from) : len(left_from) + len(right_from)]
-    (pair_ref, block_ref, w1_ref, w2_ref, out_ref, left, right, flipped, rolled, spread, stacked, middle, normed) = refs[
+    (pair_ref, block_ref, w1_ref, w2_ref, out_ref, left, right, flipped, rolled, spread, stacked, middle, normed, present) = refs[
         len(left_from) + len(right_from) :
     ]
     sequences = lefts[0].shape[0]
@@ -386,11 +392,19 @@
             c_own - shift_z + size_z, size_z
         )
         right[pl.ds(pl.multiple_of(block * sequences, sequences), sequences), :] = ref[...]
-    wide = left.shape[1] - LANES
+    wide = left.shape[1]
+    heads = biases[0].shape[0]
+    for other, ref in enumerate(biases):
+        for n in range(sequences // heads):
+            start = (z_own ^ other) * sequences + n * heads
+            mask = ref[:, ref.shape[1] - LANES :]
+            present[pl.ds(pl.multiple_of(start, heads), heads), :] = (
+                pltpu.roll(mask, LANES - n * rows, 1) if n else mask
+            )
     width = wide // rows
     fit = LANES // width
     high = wide // columns // fit
-    count = dot(right[:, wide:], left[:, wide:], (0, 0))[0:columns, :]
+    count = dot(right[:, wide:], present[...].astype(BF16), (0, 0))[0:columns, :]
     share = 1.0 / (count + 1.0)
     tiles = wide // LANES
     deep = left.shape[0]
@@ -528,12 +542,12 @@
     wq, wk, wv, wg, wr, wf, ws, bias_local = call(
         functools.partial(prepare_kernel, len(weights)),
         tuple(shape(w.shape, w.dtype) for w in weights)
-        + (shape((heads, pair_rows * pair_columns), F32),),
+        + (shape((heads, pair_rows * pair_columns + LANES), F32),),
         [pltpu.SemaphoreType.DMA((len(weights),))],
         flops=2 * 6 * pair_rows * pair_columns * pair_width * LANES,
         data=pair_rows * pair_columns * pair_width * 2,
         far=len(weights),
-    )(*weights, pair, matrix)
+    )(*weights, pair, matrix, mask)
     biases = [bias_local]
     for m in range(1, size_x):
         biases.append(lax.ppermute(bias_local, "gx", [(n, n ^ m) for n in range(size_x)]))
@@ -566,7 +580,7 @@
     message = shape((sequences, wide + LANES), BF16)
     refreshed, left_own, right_own = call(
         functools.partial(attend_kernel, heads, size_x),
-        (shape(three, BF16), message, message),
+        (shape(three, BF16), shape((sequences, wide), BF16), message),
         [
             pltpu.VMEM((size_x, heads, pair_rows * pair_columns), F32),
             pltpu.VMEM((total // LANES, residues * (heads + SKEW_SMALL), LANES), F32),
@@ -617,7 +631,7 @@
         functools.partial(pair_kernel, tuple(range(size_x)), tuple(right_from)),
         (shape(pair_features.shape, BF16),),
         [
-            pltpu.VMEM((depth, wide + LANES), BF16),
+            pltpu.VMEM((depth, wide), BF16),
             pltpu.VMEM((depth, wide + LANES), BF16),
             pltpu.VMEM((width // fit * pair_columns, fit * depth), BF16),
             pltpu.VMEM((fit - 1, depth, wide), BF16),
@@ -625,10 +639,11 @@
             pltpu.VMEM((fit, pair_rows // fit * pair_columns, width * width), BF16),
             pltpu.VMEM((fit, pair_rows // fit * pair_columns, pair_width), F32),
             pltpu.VMEM((fit, pair_rows // fit * pair_columns, pair_width), BF16),
+            pltpu.VMEM((depth, LANES), F32),
         ],
         flops=2 * pair_rows * pair_columns * width * width * pair_width * fit,
         data=width * width * fit * pair_width * fit * 2,
-    )(*lefts, *rights, pair, block, w1, w2)
+    )(*biases, *lefts, *rights, pair, block, w1, w2)
     return refreshed, pair_output
 
 

time: 40.7 us -> 45.2 us (1.11)
  waiting for transfers between devices: 13 us -> 16.8 us
  starting transfers between devices: 15.4 us -> 16 us
    ppermute x2, waiting for transfers between devices: 1.6 us -> 4.19 us  [local(): got = lax.ppermute(right_own, ('gx', 'gy', 'gz'), pairs)]
    ppermute x3, waiting for transfers between devices: 1.05 us -> 2.18 us  [local(): lax.ppermute(left_own, 'gx', [(n, n ^ m) for n in range(size_x)])]
    ppermute x5, starting transfers between devices: 3.04 us -> 3.57 us  [shift(): lax.ppermute(value, axis, [(n, (n + step) % count) for n in range(count)])]
  transfers between devices with their start and end apart: 13 -> 13, of which waited for: 5 -> 5; matrix products, arithmetic and copies ran while one was open for 0% -> 0% of each run, Pallas kernels for 11% -> 10%
where the time goes in v3:
time: 45.2 us; the launch traced here: 45 us
  waiting for transfers between devices  16.8 us (37%)
  starting transfers between devices  16 us (35%)
  Pallas kernels  11.5 us (25%)
  between operations  0.72 us (2%)
    pallas_call x7, Pallas kernels, run(): pl.pallas_call(body, out_shape=outs, in_specs=[pl.BlockSpec(memory_space=...  11.5 us
    ppermute x5, waiting for transfers between devices, shift(): lax.ppermute(value, axis, [(n, (n + step) % count) for n in range(count)])  6.49 us
    ppermute x3, starting transfers between devices, local(): lax.ppermute(bias_local, 'gx', [(n, n ^ m) for n in range(size_x)])  4.48 us
    ppermute x3, starting transfers between devices, local(): lax.ppermute(left_own, 'gx', [(n, n ^ m) for n in range(size_x)])  4.39 us
    ppermute x2, waiting for transfers between devices, local(): got = lax.ppermute(right_own, ('gx', 'gy', 'gz'), pairs)  4.19 us
    ppermute x3, waiting for transfers between devices, local(): lax.ppermute(bias_local, 'gx', [(n, n ^ m) for n in range(size_x)])  3.93 us
    ppermute x5, starting transfers between devices, shift(): lax.ppermute(value, axis, [(n, (n + step) % count) for n in range(count)])  3.57 us
    ppermute x2, starting transfers between devices, local(): got = lax.ppermute(right_own, ('gx', 'gy', 'gz'), pairs)  3.53 us
  transfers between devices with their start and end apart: 13, of which 5 were waited for; matrix products, arithmetic and copies ran while one was open for 0% of the time, Pallas kernels for 10%

profile of v3, /device:TPU:0, one launch (start us, length us, event | category | flops | bytes accessed | tf_op | source)
XLA Modules:
  0.0 45.0 jit_solution(7480791392706035205)
XLA Ops:
  0.6 1.5 %shard_map.167 = (bf16[528,256]{1,0:T(8,128)(2,1)S(1)}, f32[512,256]{1,0:T(8,128)S(1)}, s32[16,32]{1,0:T(8,128)S(1)}, bf16[32,32,128]{2,1,0:T(8,128)(2,1)S(1)}, f32[8,128]{1,0:T(8,128)S(1)}) custom-call(s32[16,32]{1,0:T(8,128)} %ids_far.1, s32[16,32]{1,0:T(8,128)} %mask_far.1, bf16[16,32,256]{2,1,0:T(8,128)(2,1)} %profile_far.1, bf16[23,256]{1,0:T(8,128)(2,1)} %table_far.1, ...), custom_call_target="tpu_custom_call" | custom-call | flops 33554432 | bytes 1048576 | tf_op jit(solution)/shard_map/pallas_call | solution.py:57
  2.2 3.0 %collective-permute-start.4 = (bf16[528,256]{1,0:T(8,128)(2,1)S(1)}, bf16[528,256]{1,0:T(8,128)(2,1)S(1)}, u32[]{:S(2)}, u32[]{:S(2)}) collective-permute-start(bf16[528,256]{1,0:T(8,128)(2,1)S(1)} %get-tuple-element.33.refs_0_), channel_id=1, source_target_pairs={{0,2},{2,0},{1,3},{3,1},{4,6},{6,4},{5,7},{7,5},{8,10},{10,8},{9,1... | collective-permute-start | bytes 811016 | tf_op jit(solution)/shard_map/ppermute | solution.py:523
  5.2 0.0 collective-permute-start.3
  5.2 6.5 %collective-permute-done.4.refs_2_ = bf16[528,256]{1,0:T(8,128)(2,1)S(1)} collective-permute-done((bf16[528,256]{1,0:T(8,128)(2,1)S(1)}, bf16[528,256]{1,0:T(8,128)(2,1)S(1)}, u32[]{:S(2)}, u32[]{:S(2)}) %collective-permute-start.4) | collective-permute-done | bytes 270368 | tf_op jit(solution)/shard_map/ppermute | solution.py:523
  11.7 0.0 collective-permute-start.5
  11.7 1.6 %shard_map.168 = (bf16[256,256]{1,0:T(8,128)(2,1)S(1)}, bf16[256,256]{1,0:T(8,128)(2,1)S(1)}, bf16[256,256]{1,0:T(8,128)(2,1)S(1)}, bf16[256,256]{1,0:T(8,128)(2...) custom-call(bf16[256,256]{1,0:T(8,128)(2,1)} %refs_0_.1, ...), custom_call_target="tpu_custom_call" | custom-call | flops 201326592 | bytes 262144 | tf_op jit(solution)/shard_map/pallas_call | solution.py:57
  13.3 1.9 %collective-permute-start = (f32[8,1152]{1,0:T(8,128)S(1)}, f32[8,1152]{1,0:T(8,128)S(1)}, u32[]{:S(2)}, u32[]{:S(2)}) collective-permute-start(f32[8,1152]{1,0:T(8,128)S(1)} %get-tuple-element.32.refs_0_), channel_id=1, source_target_pairs={{0,4},{4,0},{8,12},{12,8},{1,5},{5,1},{9,13},{13,9},{2,6},{6,2},{1... | collective-permute-start | bytes 110600 | tf_op jit(solution)/shard_map/ppermute | solution.py:553
  15.1 2.6 %collective-permute-start.1 = (f32[8,1152]{1,0:T(8,128)S(1)}, f32[8,1152]{1,0:T(8,128)S(1)}, u32[]{:S(2)}, u32[]{:S(2)}) collective-permute-start(f32[8,1152]{1,0:T(8,128)S(1)} %get-tuple-element.32.refs_0_), channel_id=1, source_target_pairs={{0,8},{4,12},{8,0},{12,4},{1,9},{5,13},{9,1},{13,5},{2,10},{6,14},... | collective-permute-start | bytes 110600 | tf_op jit(solution)/shard_map/ppermute | solution.py:553
  17.7 0.0 collective-permute-start.2
  17.7 0.0 collective-permute-done.3.refs_1_
  17.7 0.7 %shard_map.169 = (bf16[16,32,256]{2,1,0:T(8,128)(2,1)S(1)}, bf16[16,128,256]{2,1,0:T(8,128)(2,1)S(1)}, bf16[16,128,256]{2,1,0:T(8,128)(2,1)S(1)}, f32[16,32,256]{2,1,0:T(8,128)S(1)}) custom-call(bf16[528,256]{1,0:T(8,128)(2,1)S(1)} %get-tuple-element.33.refs_0_, bf16[528,256]{1,0:T(8,128)(2,1)S(1)} %collective-permute-done.3.refs_1_, ...), custom_call_target="tpu_custom_call" | custom-call | flops 536870912 | bytes 3145728 | tf_op jit(solution)/shard_map/pallas_call | solution.py:57
  18.5 0.0 collective-permute-done.5.refs_3_
  18.5 1.1 %shard_map.170 = (bf16[16,128,256]{2,1,0:T(8,128)(2,1)S(1)}, bf16[16,128,256]{2,1,0:T(8,128)(2,1)S(1)}, f32[16,256,128]{2,1,0:T(8,128)S(1)}, f32[16,128]{1,0:T(8,128)S(1)}) custom-call(bf16[528,256]{1,0:T(8,128)(2,1)S(1)} %get-tuple-element.33.refs_0_, ...), custom_call_target="tpu_custom_call", output_to_operand_aliasing={{0}: (5, {}), {1}: (6, {})} | custom-call | flops 134217728 | bytes 3145728 | tf_op jit(solution)/shard_map/pallas_call | solution.py:57
  19.6 0.0 collective-permute-done.refs_1_
  19.6 1.2 %collective-permute-done.1.refs_2_ = f32[8,1152]{1,0:T(8,128)S(1)} collective-permute-done((f32[8,1152]{1,0:T(8,128)S(1)}, f32[8,1152]{1,0:T(8,128)S(1)}, u32[]{:S(2)}, u32[]{:S(2)}) %collective-permute-start.1) | collective-permute-done | bytes 36896 | tf_op jit(solution)/shard_map/ppermute | solution.py:553
  20.7 2.8 %collective-permute-done.2.refs_3_ = f32[8,1152]{1,0:T(8,128)S(1)} collective-permute-done((f32[8,1152]{1,0:T(8,128)S(1)}, f32[8,1152]{1,0:T(8,128)S(1)}, u32[]{:S(2)}, u32[]{:S(2)}) %collective-permute-start.2) | collective-permute-done | bytes 36896 | tf_op jit(solution)/shard_map/ppermute | solution.py:553
  23.5 2.0 %shard_map.171 = (bf16[16,32,256]{2,1,0:T(8,128)(2,1)S(1)}, bf16[16,1024]{1,0:T(8,128)(2,1)S(1)}, bf16[16,1152]{1,0:T(8,128)(2,1)S(1)}) custom-call(f32[8,1152]{1,0:T(8,128)S(1)} %get-tuple-element.32.refs_0_, f32[8,1152]{1,0:T(8,128)S(1)} %collective-permute-done.refs_1_, f32[8,1152]{1,0:T(8,128)S(1)} %collective-permute-done.1.refs_2_, ...), custom_call_target="tpu_custom_call" | custom-call | flops 268435456 | bytes 2097152 | tf_op jit(solution)/shard_map/pallas_call | solution.py:57
  25.5 0.7 %collective-permute-start.9 = (bf16[16,1152]{1,0:T(8,128)(2,1)S(1)}, bf16[16,1152]{1,0:T(8,128)(2,1)S(1)}, u32[]{:S(2)}, u32[]{:S(2)}) collective-permute-start(bf16[16,1152]{1,0:T(8,128)(2,1)S(1)} %get-tuple-element.52), channel_id=1, source_target_pairs={{0,0},{1,4},{2,8},{3,12},{4,1},{5,5},{6,9},{7,13},{8,2},{9,6},{10,... | collective-permute-start | bytes 110600 | tf_op jit(solution)/shard_map/ppermute | solution.py:608
  26.2 2.9 %collective-permute-start.11 = (bf16[16,1152]{1,0:T(8,128)(2,1)S(1)}, bf16[16,1152]{1,0:T(8,128)(2,1)S(1)}, u32[]{:S(2)}, u32[]{:S(2)}) collective-permute-start(bf16[16,1152]{1,0:T(8,128)(2,1)S(1)} %get-tuple-element.52), channel_id=1, source_target_pairs={{0,2},{1,6},{2,10},{3,14},{4,3},{5,7},{6,11},{7,15},{8,0},{9,4},{1... | collective-permute-start | bytes 110600 | tf_op jit(solution)/shard_map/ppermute | solution.py:608
  29.1 0.0 collective-permute-done.9.refs_8_
  29.1 0.5 %collective-permute-start.10 = (bf16[16,1152]{1,0:T(8,128)(2,1)S(1)}, bf16[16,1152]{1,0:T(8,128)(2,1)S(1)}, u32[]{:S(2)}, u32[]{:S(2)}) collective-permute-start(bf16[16,1152]{1,0:T(8,128)(2,1)S(1)} %collective-permute-done.9.refs_8_), channel_id=1, source_target_pairs={{0,1},{1,0},{2,3},{3,2},{4,5},{5,4},{6,7},{7,6},{8,9},{9,8},{10,11... | collective-permute-start | bytes 110600 | tf_op jit(solution)/shard_map/ppermute | solution.py:523
  29.6 4.2 %collective-permute-done.11.refs_10_ = bf16[16,1152]{1,0:T(8,128)(2,1)S(1)} collective-permute-done((bf16[16,1152]{1,0:T(8,128)(2,1)S(1)}, bf16[16,1152]{1,0:T(8,128)(2,1)S(1)}, u32[]{:S(2)}, u32[]{:S(2)}) %collective-permute-start.11) | collective-permute-done | bytes 36896 | tf_op jit(solution)/shard_map/ppermute | solution.py:608
  33.8 0.0 collective-permute-start.12
  33.8 0.0 collective-permute-start.6
  33.8 2.1 %collective-permute-start.7 = (bf16[16,1024]{1,0:T(8,128)(2,1)S(1)}, bf16[16,1024]{1,0:T(8,128)(2,1)S(1)}, u32[]{:S(2)}, u32[]{:S(2)}) collective-permute-start(bf16[16,1024]{1,0:T(8,128)(2,1)S(1)} %get-tuple-element.51.refs_4_), channel_id=1, source_target_pairs={{0,8},{4,12},{8,0},{12,4},{1,9},{5,13},{9,1},{13,5},{2,10},{6,14},... | collective-permute-start | bytes 98312 | tf_op jit(solution)/shard_map/ppermute | solution.py:599
  35.9 2.3 %collective-permute-start.8 = (bf16[16,1024]{1,0:T(8,128)(2,1)S(1)}, bf16[16,1024]{1,0:T(8,128)(2,1)S(1)}, u32[]{:S(2)}, u32[]{:S(2)}) collective-permute-start(bf16[16,1024]{1,0:T(8,128)(2,1)S(1)} %get-tuple-element.51.refs_4_), channel_id=1, source_target_pairs={{0,12},{4,8},{8,4},{12,0},{1,13},{5,9},{9,5},{13,1},{2,14},{6,10},... | collective-permute-start | bytes 98312 | tf_op jit(solution)/shard_map/ppermute | solution.py:599
  38.2 1.2 %shard_map.172 = (bf16[4,1024,128]{2,1,0:T(8,128)(2,1)S(1)}, bf16[128,512]{1,0:T(8,128)(2,1)S(1)}, bf16[512,128]{1,0:T(8,128)(2,1)S(1)}, bf16[16,32,256]{2,1,0:T(8,128)(2,1)}) custom-call(bf16[1024,128]{1,0:T(8,128)(2,1)} %mix_far.1, bf16[128,512]{1,0:T(8,128)(2,1)} %w1_far.1, bf16[512,128]{1,0:T(8,128)(2,1)} %w2_far.1, ...), custom_call_target="tpu_custom_call" | custom-call | bytes 1048576 | tf_op jit(solution)/shard_map/pallas_call | solution.py:57
  39.4 0.0 collective-permute-done.6.refs_5_
  39.4 2.2 %collective-permute-done.8.refs_7_ = bf16[16,1024]{1,0:T(8,128)(2,1)S(1)} collective-permute-done((bf16[16,1024]{1,0:T(8,128)(2,1)S(1)}, bf16[16,1024]{1,0:T(8,128)(2,1)S(1)}, u32[]{:S(2)}, u32[]{:S(2)}) %collective-permute-start.8) | collective-permute-done | bytes 32800 | tf_op jit(solution)/shard_map/ppermute | solution.py:599
  41.6 0.0 collective-permute-done.10.refs_9_
  41.6 0.0 collective-permute-done.12.refs_11_
  41.6 3.4 %shard_map.173 = bf16[32,32,128]{2,1,0:T(8,128)(2,1)} custom-call(f32[8,1152]{1,0:T(8,128)S(1)} %get-tuple-element.32.refs_0_, f32[8,1152]{1,0:T(8,128)S(1)} %collective-permute-done.refs_1_, f32[8,1152]{1,0:T(8,128)S(1)} %collective-permute-done.1.refs_2_, f32[8,1152]{1,0:T(8,128)S(1)} %collective-permute-done.2.refs_3_, ...), custom_call_target="tpu_custom_call" | custom-call | flops 1073741824 | bytes 4194304 | tf_op jit(solution)/shard_map/pallas_call | solution.py:57
  (1 shorter events, 0.0 us)
Async XLA Ops:
  2.2 9.5 %collective-permute-start.4 = (bf16[528,256]{1,0:T(8,128)(2,1)S(1)}, bf16[528,256]{1,0:T(8,128)(2,1)S(1)}, u32[]{:S(2)}, u32[]{:S(2)}) collective-permute-start(bf16[528,256]{1,0:T(8,128)(2,1)S(1)} %get-tuple-element.33.refs_0_), channel_id=1, source_target_pairs={{0,2},{2,0},{1,3},{3,1},{4,6},{6,4},{5,7},{7,5},{8,10},{10,8},{9,1... | collective-permute-start | bytes 811016 | tf_op jit(solution)/shard_map/ppermute | solution.py:523
  5.2 12.6 %collective-permute-start.3 = (bf16[528,256]{1,0:T(8,128)(2,1)S(1)}, bf16[528,256]{1,0:T(8,128)(2,1)S(1)}, u32[]{:S(2)}, u32[]{:S(2)}) collective-permute-start(bf16[528,256]{1,0:T(8,128)(2,1)S(1)} %get-tuple-element.33.refs_0_), channel_id=1, source_target_pairs={{0,1},{1,0},{2,3},{3,2},{4,5},{5,4},{6,7},{7,6},{8,9},{9,8},{10,11... | collective-permute-start | bytes 811016 | tf_op jit(solution)/shard_map/ppermute | solution.py:523
  11.7 6.8 %collective-permute-start.5 = (bf16[528,256]{1,0:T(8,128)(2,1)S(1)}, bf16[528,256]{1,0:T(8,128)(2,1)S(1)}, u32[]{:S(2)}, u32[]{:S(2)}) collective-permute-start(bf16[528,256]{1,0:T(8,128)(2,1)S(1)} %collective-permute-done.4.refs_2_), channel_id=1, source_target_pairs={{0,1},{1,0},{2,3},{3,2},{4,5},{5,4},{6,7},{7,6},{8,9},{9,8},{10,11... | collective-permute-start | bytes 811016 | tf_op jit(solution)/shard_map/ppermute | solution.py:523
  13.3 6.3 %collective-permute-start = (f32[8,1152]{1,0:T(8,128)S(1)}, f32[8,1152]{1,0:T(8,128)S(1)}, u32[]{:S(2)}, u32[]{:S(2)}) collective-permute-start(f32[8,1152]{1,0:T(8,128)S(1)} %get-tuple-element.32.refs_0_), channel_id=1, source_target_pairs={{0,4},{4,0},{8,12},{12,8},{1,5},{5,1},{9,13},{13,9},{2,6},{6,2},{1... | collective-permute-start | bytes 110600 | tf_op jit(solution)/shard_map/ppermute | solution.py:553
  15.1 5.6 %collective-permute-start.1 = (f32[8,1152]{1,0:T(8,128)S(1)}, f32[8,1152]{1,0:T(8,128)S(1)}, u32[]{:S(2)}, u32[]{:S(2)}) collective-permute-start(f32[8,1152]{1,0:T(8,128)S(1)} %get-tuple-element.32.refs_0_), channel_id=1, source_target_pairs={{0,8},{4,12},{8,0},{12,4},{1,9},{5,13},{9,1},{13,5},{2,10},{6,14},... | collective-permute-start | bytes 110600 | tf_op jit(solution)/shard_map/ppermute | solution.py:553
  17.7 5.8 %collective-permute-start.2 = (f32[8,1152]{1,0:T(8,128)S(1)}, f32[8,1152]{1,0:T(8,128)S(1)}, u32[]{:S(2)}, u32[]{:S(2)}) collective-permute-start(f32[8,1152]{1,0:T(8,128)S(1)} %get-tuple-element.32.refs_0_), channel_id=1, source_target_pairs={{0,12},{4,8},{8,4},{12,0},{1,13},{5,9},{9,5},{13,1},{2,14},{6,10},... | collective-permute-start | bytes 110600 | tf_op jit(solution)/shard_map/ppermute | solution.py:553
  25.5 3.5 %collective-permute-start.9 = (bf16[16,1152]{1,0:T(8,128)(2,1)S(1)}, bf16[16,1152]{1,0:T(8,128)(2,1)S(1)}, u32[]{:S(2)}, u32[]{:S(2)}) collective-permute-start(bf16[16,1152]{1,0:T(8,128)(2,1)S(1)} %get-tuple-element.52), channel_id=1, source_target_pairs={{0,0},{1,4},{2,8},{3,12},{4,1},{5,5},{6,9},{7,13},{8,2},{9,6},{10,... | collective-permute-start | bytes 110600 | tf_op jit(solution)/shard_map/ppermute | solution.py:608
  26.2 7.6 %collective-permute-start.11 = (bf16[16,1152]{1,0:T(8,128)(2,1)S(1)}, bf16[16,1152]{1,0:T(8,128)(2,1)S(1)}, u32[]{:S(2)}, u32[]{:S(2)}) collective-permute-start(bf16[16,1152]{1,0:T(8,128)(2,1)S(1)} %get-tuple-element.52), channel_id=1, source_target_pairs={{0,2},{1,6},{2,10},{3,14},{4,3},{5,7},{6,11},{7,15},{8,0},{9,4},{1... | collective-permute-start | bytes 110600 | tf_op jit(solution)/shard_map/ppermute | solution.py:608
  29.1 12.5 %collective-permute-start.10 = (bf16[16,1152]{1,0:T(8,128)(2,1)S(1)}, bf16[16,1152]{1,0:T(8,128)(2,1)S(1)}, u32[]{:S(2)}, u32[]{:S(2)}) collective-permute-start(bf16[16,1152]{1,0:T(8,128)(2,1)S(1)} %collective-permute-done.9.refs_8_), channel_id=1, source_target_pairs={{0,1},{1,0},{2,3},{3,2},{4,5},{5,4},{6,7},{7,6},{8,9},{9,8},{10,11... | collective-permute-start | bytes 110600 | tf_op jit(solution)/shard_map/ppermute | solution.py:523
  33.8 7.8 %collective-permute-start.12 = (bf16[16,1152]{1,0:T(8,128)(2,1)S(1)}, bf16[16,1152]{1,0:T(8,128)(2,1)S(1)}, u32[]{:S(2)}, u32[]{:S(2)}) collective-permute-start(bf16[16,1152]{1,0:T(8,128)(2,1)S(1)} %collective-permute-done.11.refs_10_), channel_id=1, source_target_pairs={{0,1},{1,0},{2,3},{3,2},{4,5},{5,4},{6,7},{7,6},{8,9},{9,8},{10,11... | collective-permute-start | bytes 110600 | tf_op jit(solution)/shard_map/ppermute | solution.py:523
  33.8 5.6 %collective-permute-start.6 = (bf16[16,1024]{1,0:T(8,128)(2,1)S(1)}, bf16[16,1024]{1,0:T(8,128)(2,1)S(1)}, u32[]{:S(2)}, u32[]{:S(2)}) collective-permute-start(bf16[16,1024]{1,0:T(8,128)(2,1)S(1)} %get-tuple-element.51.refs_4_), channel_id=1, source_target_pairs={{0,4},{4,0},{8,12},{12,8},{1,5},{5,1},{9,13},{13,9},{2,6},{6,2},{1... | collective-permute-start | bytes 98312 | tf_op jit(solution)/shard_map/ppermute | solution.py:599
  33.8 5.6 %collective-permute-start.7 = (bf16[16,1024]{1,0:T(8,128)(2,1)S(1)}, bf16[16,1024]{1,0:T(8,128)(2,1)S(1)}, u32[]{:S(2)}, u32[]{:S(2)}) collective-permute-start(bf16[16,1024]{1,0:T(8,128)(2,1)S(1)} %get-tuple-element.51.refs_4_), channel_id=1, source_target_pairs={{0,8},{4,12},{8,0},{12,4},{1,9},{5,13},{9,1},{13,5},{2,10},{6,14},... | collective-permute-start | bytes 98312 | tf_op jit(solution)/shard_map/ppermute | solution.py:599
  35.9 5.7 %collective-permute-start.8 = (bf16[16,1024]{1,0:T(8,128)(2,1)S(1)}, bf16[16,1024]{1,0:T(8,128)(2,1)S(1)}, u32[]{:S(2)}, u32[]{:S(2)}) collective-permute-start(bf16[16,1024]{1,0:T(8,128)(2,1)S(1)} %get-tuple-element.51.refs_4_), channel_id=1, source_target_pairs={{0,12},{4,8},{8,4},{12,0},{1,13},{5,9},{9,5},{13,1},{2,14},{6,10},... | collective-permute-start | bytes 98312 | tf_op jit(solution)/shard_map/ppermute | solution.py:599
